TPU v7x, 32 devices: a whole 2x2x4 slice. The times are simulated.
32 devices in a mesh: dp: 16 (over z, y, core), tensor: 2 (over x).
Axes of the slice: x: 2, y: 2, z: 4, core: 2. Of those that a mesh axis runs over, the one named last changes fastest.
Arguments:
- tokens: bfloat16 [16384, 1024], P(('dp', 'tensor')), may hold values from -6 to 6
- doc_ids: int32 [16384], P('dp'), may hold values from 0 to 4, as said below
- w_qkv: bfloat16 [3, 1024, 1024], P(None, None, 'tensor'), may hold values from -0.1875 to 0.1875
- qv_bias: float32 [2, 1024], P(None, 'tensor'), may hold values from -3 to 3
- out_weight: bfloat16 [1024, 1024], P('tensor'), may hold values from -3 to 3
- out_biases: float32 [2, 1024], replicated, may hold values from -3 to 3
- ln_gains: float32 [2, 1024], replicated, may hold values from 0.1 to 1.9
- ln_shifts: float32 [2, 1024], replicated, may hold values from -3 to 3
- up_weight: bfloat16 [1024, 4096], P(None, 'tensor'), may hold values from -0.1875 to 0.1875
- up_bias: float32 [4096], P('tensor'), may hold values from -3 to 3
- down_weight: bfloat16 [4096, 1024], P('tensor'), may hold values from -0.09375 to 0.09375
- cotangent: bfloat16 [16384, 1024], P(('dp', 'tensor')), may hold values from -6 to 6
Outputs:
- out: bfloat16 [16384, 1024], P(('dp', 'tensor'))
- grad_input: bfloat16 [16384, 1024], P(('dp', 'tensor'))
- grad_qkv: float32 [3, 1024, 1024], P(None, None, 'tensor')
- grad_qv_bias: float32 [2, 1024], P(None, 'tensor')
- grad_out_weight: float32 [1024, 1024], P('tensor')
- grad_out_biases: float32 [2, 1024], replicated
- grad_ln_gains: float32 [2, 1024], replicated
- grad_ln_shifts: float32 [2, 1024], replicated
- grad_up_weight: float32 [1024, 4096], P(None, 'tensor')
- grad_up_bias: float32 [4096], P('tensor')
- grad_down_weight: float32 [4096, 1024], P('tensor')
Inputs may be any that keep to these rules, and one draw needn't show every extreme that they name: `doc_ids`: within each buffer (rows 1024 * b to 1024 * (b + 1) - 1) the numbers never fall; the value 4 marks padding, which stands only at a buffer's end; at least 512 slots of every buffer are not padding; a sequence is a run of one number below 4 in one buffer, of 1 to 1024 slots, and some buffer holds a single sequence of 1024 slots.
All inputs are finite; a program needn't handle non-finite values.
Results may differ from a plain program's by a relative error of at most 0.03.
Values may be sent and summed in bfloat16 or wider, within the bound.
No kernel may reach another device: no remote copies, remote signals or barrier semaphores. Data moves between devices by JAX's collectives and lax.ppermute only.
A program may use at most 256 MiB of HBM per device.

v0:
```python
import math

import jax
import jax.numpy as jnp
from jax import lax
from jax.sharding import PartitionSpec as P

D = 1024
H = 16
DOCS_DEV = 4


EPSILON = 1e-06
ROOT_HALF = 0.7071067811865476
GAUSS_NORM = 0.3989422804014327


def norm_forward(summed, gain, shift):
    centred = summed - jnp.mean(summed, axis=-1, keepdims=True)
    inverse = lax.rsqrt(jnp.mean(centred * centred, axis=-1, keepdims=True) + EPSILON)
    unit = centred * inverse
    return (unit * gain + shift, unit, inverse)


def norm_backward(upstream, unit, inverse, gain):
    spread = upstream * gain
    inner = (
        spread
        - jnp.mean(spread, axis=-1, keepdims=True)
        - unit * jnp.mean(spread * unit, axis=-1, keepdims=True)
    )
    return (inner * inverse, jnp.sum(upstream * unit, axis=0), jnp.sum(upstream, axis=0))


def gelu_slope(hidden):
    return (
        0.5 * (1.0 + lax.erf(hidden * ROOT_HALF))
        + hidden * jnp.exp(-0.5 * hidden * hidden) * GAUSS_NORM
    )


def masked_scores(query_rows, keys_all, doc_rows, doc_all, score_scale):
    scores = (
        jnp.einsum("qhc,khc->hqk", query_rows, keys_all, preferred_element_type=jnp.float32)
        * score_scale
    )
    allowed = doc_rows[:, None] == doc_all[None, :]
    return jnp.where(allowed[None], scores, -1000000000.0)


def attention_forward(queries, keys_all, values_all, doc_all, block_rows, score_scale):
    block_count = queries.shape[0] // block_rows

    def one_block(block_index):
        first_row = block_index * block_rows
        query_rows = lax.dynamic_slice_in_dim(queries, first_row, block_rows, 0)
        doc_rows = lax.dynamic_slice_in_dim(doc_all, first_row, block_rows, 0)
        scores = masked_scores(query_rows, keys_all, doc_rows, doc_all, score_scale)
        row_max = jnp.max(scores, axis=-1, keepdims=True)
        expd = jnp.exp(scores - row_max)
        row_sum = jnp.sum(expd, axis=-1, keepdims=True)
        weights_low = (expd / row_sum).astype(jnp.bfloat16)
        mixed_heads = jnp.einsum(
            "hqk,khc->qhc", weights_low, values_all, preferred_element_type=jnp.float32
        )
        return (mixed_heads, row_max[..., 0] + jnp.log(row_sum[..., 0]))

    mixed_heads, log_sums = lax.map(one_block, jnp.arange(block_count, dtype=jnp.int32))
    return (mixed_heads.reshape(queries.shape[0], -1), log_sums)


def attention_backward(
    queries, keys_all, values_all, doc_all, log_sums, grad_mixed, block_rows, score_scale
):
    block_count = queries.shape[0] // block_rows

    def one_block(running, block_index):
        key_grad, value_grad = running
        first_row = block_index * block_rows
        query_rows = lax.dynamic_slice_in_dim(queries, first_row, block_rows, 0)
        doc_rows = lax.dynamic_slice_in_dim(doc_all, first_row, block_rows, 0)
        grad_rows = lax.dynamic_slice_in_dim(grad_mixed, first_row, block_rows, 0)
        scores = masked_scores(query_rows, keys_all, doc_rows, doc_all, score_scale)
        probs_all = jnp.exp(scores - log_sums[block_index][:, :, None])
        value_grad = value_grad + jnp.einsum(
            "hqk,qhc->khc",
            probs_all.astype(jnp.bfloat16),
            grad_rows,
            preferred_element_type=jnp.float32,
        )
        prob_grad = jnp.einsum(
            "qhc,khc->hqk", grad_rows, values_all, preferred_element_type=jnp.float32
        )
        score_grad = probs_all * (
            prob_grad - jnp.sum(probs_all * prob_grad, axis=-1, keepdims=True)
        )
        score_low = score_grad.astype(jnp.bfloat16)
        query_grad = (
            jnp.einsum("hqk,khc->qhc", score_low, keys_all, preferred_element_type=jnp.float32)
            * score_scale
        )
        key_grad = (
            key_grad
            + jnp.einsum("hqk,qhc->khc", score_low, query_rows, preferred_element_type=jnp.float32)
            * score_scale
        )
        return ((key_grad, value_grad), query_grad)

    zeros_like_keys = jnp.zeros(keys_all.shape, jnp.float32)
    (key_grad, value_grad), query_grad = lax.scan(
        one_block, (zeros_like_keys, zeros_like_keys), jnp.arange(block_count, dtype=jnp.int32)
    )
    return (query_grad.reshape(keys_all.shape), key_grad, value_grad)


def shards(
    tokens,
    doc_ids,
    w_qkv,
    qv_bias,
    out_weight,
    out_biases,
    ln_gains,
    ln_shifts,
    up_weight,
    up_bias,
    down_weight,
    cotangent,
):
    rows_own = tokens.shape[0]
    gathered = lax.all_gather(tokens, "tensor", axis=0, tiled=True)
    row_total = gathered.shape[0]
    head_size = D // H
    local_width = w_qkv.shape[2]
    local_heads = local_width // head_size
    block_rows = min(512, row_total)
    score_scale = 1.0 / math.sqrt(head_size)
    tensor_pos = lax.axis_index("tensor")
    projected = jnp.einsum("sd,idc->isc", gathered, w_qkv, preferred_element_type=jnp.float32)
    queries = (
        (projected[0] + qv_bias[0]).astype(jnp.bfloat16).reshape(row_total, local_heads, head_size)
    )
    keys_all = projected[1].astype(jnp.bfloat16).reshape(row_total, local_heads, head_size)
    values_all = (
        (projected[2] + qv_bias[1]).astype(jnp.bfloat16).reshape(row_total, local_heads, head_size)
    )
    mixed_heads, log_sums = attention_forward(
        queries, keys_all, values_all, doc_ids, block_rows, score_scale
    )
    mixed_low = mixed_heads.astype(jnp.bfloat16)
    attention = lax.psum_scatter(
        jnp.dot(mixed_low, out_weight, preferred_element_type=jnp.float32).astype(jnp.bfloat16),
        "tensor",
        scatter_dimension=0,
        tiled=True,
    ).astype(jnp.float32)
    inputs_own = tokens.astype(jnp.float32)
    normed, unit_first, inverse_first = norm_forward(
        inputs_own + attention + out_biases[0], ln_gains[0], ln_shifts[0]
    )
    normed_all = lax.all_gather(normed.astype(jnp.bfloat16), "tensor", axis=0, tiled=True)
    hidden = jnp.dot(normed_all, up_weight, preferred_element_type=jnp.float32) + up_bias
    active_low = jax.nn.gelu(hidden, approximate=False).astype(jnp.bfloat16)
    branch = lax.psum_scatter(
        jnp.dot(active_low, down_weight, preferred_element_type=jnp.float32).astype(jnp.bfloat16),
        "tensor",
        scatter_dimension=0,
        tiled=True,
    ).astype(jnp.float32)
    result, unit_second, inverse_second = norm_forward(
        normed + branch + out_biases[1], ln_gains[1], ln_shifts[1]
    )
    doc_own = lax.dynamic_slice_in_dim(doc_ids, tensor_pos * rows_own, rows_own, 0)
    out_grad = cotangent.astype(jnp.float32) * (doc_own < DOCS_DEV).astype(jnp.float32)[:, None]
    second_grad, gain_grad_second, shift_grad_second = norm_backward(
        out_grad, unit_second, inverse_second, ln_gains[1]
    )
    bias_grad_second = jnp.sum(second_grad, axis=0)
    branch_grad = lax.all_gather(second_grad.astype(jnp.bfloat16), "tensor", axis=0, tiled=True)
    grad_down = jnp.einsum("sf,sd->fd", active_low, branch_grad, preferred_element_type=jnp.float32)
    active_grad = jnp.einsum(
        "sd,fd->sf", branch_grad, down_weight, preferred_element_type=jnp.float32
    )
    hidden_low = (active_grad * gelu_slope(hidden)).astype(jnp.bfloat16)
    grad_up_bias = jnp.sum(hidden_low.astype(jnp.float32), axis=0)
    grad_up = jnp.einsum("sd,sf->df", normed_all, hidden_low, preferred_element_type=jnp.float32)
    normed_grad = second_grad + lax.psum_scatter(
        jnp.einsum("sf,df->sd", hidden_low, up_weight, preferred_element_type=jnp.float32).astype(
            jnp.bfloat16
        ),
        "tensor",
        scatter_dimension=0,
        tiled=True,
    ).astype(jnp.float32)
    first_grad, gain_grad_first, shift_grad_first = norm_backward(
        normed_grad, unit_first, inverse_first, ln_gains[0]
    )
    bias_grad_first = jnp.sum(first_grad, axis=0)
    attn_grad = lax.all_gather(first_grad.astype(jnp.bfloat16), "tensor", axis=0, tiled=True)
    grad_out = jnp.einsum("sc,sd->cd", mixed_low, attn_grad, preferred_element_type=jnp.float32)
    mixed_grad = jnp.einsum(
        "sd,cd->sc", attn_grad, out_weight, preferred_element_type=jnp.float32
    ).astype(jnp.bfloat16)
    mixed_grad = mixed_grad.reshape(row_total, local_heads, head_size)
    query_grad, key_grad, value_grad = attention_backward(
        queries, keys_all, values_all, doc_ids, log_sums, mixed_grad, block_rows, score_scale
    )
    qkv_grad = (
        jnp.stack([query_grad, key_grad, value_grad])
        .reshape(3, row_total, local_width)
        .astype(jnp.bfloat16)
    )
    grad_qkv = jnp.einsum("sd,isc->idc", gathered, qkv_grad, preferred_element_type=jnp.float32)
    qkv_sums = jnp.sum(qkv_grad.astype(jnp.float32), axis=1)
    grad_qv = jnp.stack([qkv_sums[0], qkv_sums[2]])
    grad_input = (
        first_grad
        + lax.psum_scatter(
            jnp.einsum("isc,idc->sd", qkv_grad, w_qkv, preferred_element_type=jnp.float32).astype(
                jnp.bfloat16
            ),
            "tensor",
            scatter_dimension=0,
            tiled=True,
        ).astype(jnp.float32)
    ).astype(jnp.bfloat16)
    shared_terms = jnp.stack(
        [
            bias_grad_first,
            bias_grad_second,
            gain_grad_first,
            gain_grad_second,
            shift_grad_first,
            shift_grad_second,
        ]
    )
    shared = lax.psum(shared_terms, ("dp", "tensor"))
    grad_qkv, grad_qv, grad_out, grad_up, grad_up_bias, grad_down = (
        lax.psum(grad_qkv.astype(jnp.bfloat16), "dp").astype(jnp.float32),
        lax.psum(grad_qv.astype(jnp.bfloat16), "dp").astype(jnp.float32),
        lax.psum(grad_out.astype(jnp.bfloat16), "dp").astype(jnp.float32),
        lax.psum(grad_up.astype(jnp.bfloat16), "dp").astype(jnp.float32),
        lax.psum(grad_up_bias.astype(jnp.bfloat16), "dp").astype(jnp.float32),
        lax.psum(grad_down.astype(jnp.bfloat16), "dp").astype(jnp.float32),
    )
    return (
        result.astype(jnp.bfloat16),
        grad_input,
        grad_qkv,
        grad_qv,
        grad_out,
        shared[0:2],
        shared[2:4],
        shared[4:6],
        grad_up,
        grad_up_bias,
        grad_down,
    )


def solution(mesh):
    placed = (
        P(("dp", "tensor"), None),
        P("dp"),
        P(None, None, "tensor"),
        P(None, "tensor"),
        P("tensor", None),
        P(),
        P(),
        P(),
        P(None, "tensor"),
        P("tensor"),
        P("tensor", None),
        P(("dp", "tensor"), None),
    )
    return jax.shard_map(
        shards,
        mesh=mesh,
        in_specs=placed,
        out_specs=(
            P(("dp", "tensor"), None),
            P(("dp", "tensor"), None),
            P(None, None, "tensor"),
            P(None, "tensor"),
            P("tensor", None),
            P(),
            P(),
            P(),
            P(None, "tensor"),
            P("tensor"),
            P("tensor", None),
        ),
        check_vma=False,
    )
```

profile of v0, /device:TPU:0, one launch (start us, length us, event | category | flops | bytes accessed | tf_op | source)
XLA Modules:
  0.0 812.9 jit_solution(3118124753312838614)
XLA Ops:
  9.0 36.4 %all-gather.5.cloned.1.call-done = bf16[1024,1024]{1,0:T(8,128)(2,1)} async-done(((bf16[512,1024]{1,0:T(8,128)(2,1)}), bf16[1024,1024]{1,0:T(8,128)(2,1)}) %all-gather.5.cloned.1.call-update) | async-done | bytes 2097168 | tf_op jit(solution)/shard_map/all_gather | solution.py:131
  55.0 34.4 %while.27 = (s32[]{:T(128)}, bf16[2,512,8,64]{1,3,2,0:T(8,128)(2,1)}, f32[2,8,512]{2,1,0:T(8,128)S(1)}, s32[2]{0:T(128)S(1)}, s32[1024]{0:T(1024)S(1)}, /*index=...) while((s32[]{:T(128)}, ...), condition=%wide.region_3.4_spmd, body=%wide.region_0.3_spmd.sunk | while | flops 1124593664 | bytes 68823320 | solution.py:68
  96.0 31.6 %reduce-scatter.5.cloned.1.call-done = bf16[512,1024]{1,0:T(8,128)(2,1)} async-done(((bf16[1024,1024]{1,0:T(8,128)(2,1)}), bf16[512,1024]{1,0:T(8,128)(2,1)}) %reduce-scatter.5.cloned.1.call-update) | async-done | bytes 1048592 | tf_op jit(solution)/shard_map/reduce_scatter | solution.py:151
  133.5 33.2 %all-gather.7.cloned.1.call-done = bf16[1024,1024]{1,0:T(8,128)(2,1)} async-done(((bf16[512,1024]{1,0:T(8,128)(2,1)}), bf16[1024,1024]{1,0:T(8,128)(2,1)}) %all-gather.7.cloned.1.call-update) | async-done | bytes 2097168 | tf_op jit(solution)/shard_map/all_gather | solution.py:161
  166.8 25.3 %fusion.27 = (bf16[1024,2048]{1,0:T(8,128)(2,1)S(1)}, f32[1024,2048]{1,0:T(8,128)}) fusion(f32[2048]{0:T(1024)S(1)} %copy-done.44, bf16[1024,1024]{1,0:T(8,128)(2,1)} %all-gather.7.cloned.1.call-done, bf16[1024,2048]{1,0:T(8,128)(2,1)} %param.24), kind=kOutput, calls=%fused_computation.40 | convolution fusion | flops 4433379328 | bytes 18882560 | tf_op jit(solution)/shard_map/dot_general | solution.py:162
  200.3 31.5 %reduce-scatter.7.cloned.1.call-done = bf16[512,1024]{1,0:T(8,128)(2,1)} async-done(((bf16[1024,1024]{1,0:T(8,128)(2,1)}), bf16[512,1024]{1,0:T(8,128)(2,1)}) %reduce-scatter.7.cloned.1.call-update) | async-done | bytes 1048592 | tf_op jit(solution)/shard_map/reduce_scatter | solution.py:164
  239.3 33.2 %all-gather.9.cloned.1.call-done = bf16[1024,1024]{1,0:T(8,128)(2,1)} async-done(((bf16[512,1024]{1,0:T(8,128)(2,1)}), bf16[1024,1024]{1,0:T(8,128)(2,1)}) %all-gather.9.cloned.1.call-update) | async-done | bytes 2097168 | tf_op jit(solution)/shard_map/all_gather | solution.py:179
  272.6 11.5 %fusion.60 = (bf16[2048]{0:T(1024)(128)(2,1)}, bf16[1024,2048]{1,0:T(8,128)(2,1)S(1)}) fusion(f32[1024,2048]{1,0:T(8,128)} %get-tuple-element.256, f32[2048]{0:T(1024)S(1)} %copy-done.44, bf16[1024,1024]{1,0:T(8,128)(2,1)} %all-gather.9.cloned.1.call-done, bf16[2048,1024]{1,0:T(8,128)(2,1)} %param.26), kind=kOutput, calls=%fused_computation.125 | convolution fusion | flops 4320131072 | bytes 18886656 | tf_op jit(solution)/shard_map/sd,fd->sf/dot_general | solution.py:181
  291.8 31.9 %reduce-scatter.9.cloned.1.call-done = bf16[512,1024]{1,0:T(8,128)(2,1)} async-done(((bf16[1024,1024]{1,0:T(8,128)(2,1)}), bf16[512,1024]{1,0:T(8,128)(2,1)}) %reduce-scatter.9.cloned.1.call-update) | async-done | bytes 1048592 | tf_op jit(solution)/shard_map/reduce_scatter | solution.py:187
  332.6 33.2 %all-gather.11.cloned.1.call-done = bf16[1024,1024]{1,0:T(8,128)(2,1)} async-done(((bf16[512,1024]{1,0:T(8,128)(2,1)}), bf16[1024,1024]{1,0:T(8,128)(2,1)}) %all-gather.11.cloned.1.call-update) | async-done | bytes 2097168 | tf_op jit(solution)/shard_map/all_gather | solution.py:199
  371.0 117.0 %while.28 = (s32[]{:T(128)}, f32[1024,8,64]{0,2,1:T(8,128)}, f32[1024,8,64]{0,2,1:T(8,128)}, bf16[2,512,8,64]{1,3,2,0:T(8,128)(2,1)}, s32[2]{0:T(128)S(1)}, /*in...) while((s32[]{:T(128)}, f32[1024,8,64]{0,2,1:T(8,128)}, ...), condition=%wide.region_17.18_spmd.clone, body=%wide.region_15.17_spmd.clone.sunk | while | flops 2725507072 | bytes 271673792 | solution.py:110
  374.8 9.6 %fusion.118 = f32[8,512,1024]{2,1,0:T(8,128)} fusion(bf16[1024,8,64]{0,2,1:T(8,128)(2,1)} %get-tuple-element.463, bf16[1024,8,64]{0,2,1:T(8,128)(2,1)} %get-tuple-element.462, s32[]{:T(128)S(6)} %select_n.51), kind=kOutput, calls=%fused_computation.27.clone.1 | convolution fusion | flops 536870912 | bytes 18350084 | tf_op jit(solution)/shard_map/while/body/eval_jaxpr/qhc,khc->hqk/dot_general | solution.py:91
  384.5 12.5 %multiply_reduce_fusion.9 = (f32[8,512]{1,0:T(8,128)S(1)}, f32[8,512,1024]{2,1,0:T(8,128)}) fusion(f32[8,512,1024]{2,1,0:T(8,128)} %fusion.118, f32[8,512]{1,0:T(8,128)S(1)} %dynamic-slice_bitcast_fusion.2, bf16[1024,8,64]{0,2,1:T(8,128)(2,1)S(1)} %copy-done.3, bf16[1024,8,64]{0,2,1:T(8,128)(2,1)S(1)} %copy-done.7, s32[]{:T(128)S(6)} %select_n.51, ...), kind=kOutput, calls=%fused_computation.16.clone.1 | convolution fusion | flops 557838336 | bytes 35684356 | tf_op jit(solution)/shard_map/while/body/eval_jaxpr/qhc,khc->hqk/dot_general | solution.py:44
  397.0 15.0 %multiply_convert_fusion.2 = bf16[8,512,1024]{2,1,0:T(8,128)(2,1)} fusion(f32[8,512,1024]{2,1,0:T(8,128)} %get-tuple-element.383, f32[8,512,1024]{2,1,0:T(8,128)} %fusion.118, f32[8,512]{1,0:T(8,128)S(1)} %get-tuple-element.384), kind=kLoop, calls=%fused_computation.15.clone.1 | loop fusion | flops 12582912 | bytes 41959424 | tf_op jit(solution)/shard_map/while/body/eval_jaxpr/convert_element_type | solution.py:97
  418.5 7.0 fusion.119
  432.4 9.6 %fusion.118 = f32[8,512,1024]{2,1,0:T(8,128)} fusion(bf16[1024,8,64]{0,2,1:T(8,128)(2,1)} %get-tuple-element.463, bf16[1024,8,64]{0,2,1:T(8,128)(2,1)} %get-tuple-element.462, s32[]{:T(128)S(6)} %select_n.51), kind=kOutput, calls=%fused_computation.27.clone.1 | convolution fusion | flops 536870912 | bytes 18350084 | tf_op jit(solution)/shard_map/while/body/eval_jaxpr/qhc,khc->hqk/dot_general | solution.py:91
  442.0 12.5 %multiply_reduce_fusion.9 = (f32[8,512]{1,0:T(8,128)S(1)}, f32[8,512,1024]{2,1,0:T(8,128)}) fusion(f32[8,512,1024]{2,1,0:T(8,128)} %fusion.118, f32[8,512]{1,0:T(8,128)S(1)} %dynamic-slice_bitcast_fusion.2, bf16[1024,8,64]{0,2,1:T(8,128)(2,1)S(1)} %copy-done.3, bf16[1024,8,64]{0,2,1:T(8,128)(2,1)S(1)} %copy-done.7, s32[]{:T(128)S(6)} %select_n.51, ...), kind=kOutput, calls=%fused_computation.16.clone.1 | convolution fusion | flops 557838336 | bytes 35684356 | tf_op jit(solution)/shard_map/while/body/eval_jaxpr/qhc,khc->hqk/dot_general | solution.py:44
  454.6 15.0 %multiply_convert_fusion.2 = bf16[8,512,1024]{2,1,0:T(8,128)(2,1)} fusion(f32[8,512,1024]{2,1,0:T(8,128)} %get-tuple-element.383, f32[8,512,1024]{2,1,0:T(8,128)} %fusion.118, f32[8,512]{1,0:T(8,128)S(1)} %get-tuple-element.384), kind=kLoop, calls=%fused_computation.15.clone.1 | loop fusion | flops 12582912 | bytes 41959424 | tf_op jit(solution)/shard_map/while/body/eval_jaxpr/convert_element_type | solution.py:97
  477.8 7.0 fusion.119
  512.4 9.6 %convolution_convert_fusion = bf16[2048,1024]{1,0:T(8,128)(2,1)} fusion(bf16[1024,2048]{1,0:T(8,128)(2,1)} %copy-done.47, bf16[1024,1024]{1,0:T(8,128)(2,1)} %all-gather.9.cloned.1.call-done), kind=kOutput, calls=%fused_computation.63 | convolution fusion | flops 4297064448 | bytes 10485760 | tf_op jit(solution)/shard_map/sf,sd->fd/dot_general | solution.py:180
  536.7 40.8 %psum.52 = f32[6,1024]{1,0:T(8,128)S(1)} all-reduce(f32[6,1024]{1,0:T(8,128)S(1)} %stack.47), channel_id=1, replica_groups=mesh['dp'=16,'tensor'=2] {'dp','tensor'}, use_global_device_ids=true, to_apply=%region_29.30 | all-reduce | flops 6144 | bytes 49152 | tf_op jit(solution)/shard_map/psum | solution.py:237
  580.6 35.1 %all-reduce = (bf16[2,512]{1,0:T(2,128)(2,1)S(1)}, bf16[2048]{0:T(1024)(128)(2,1)S(1)}) all-reduce(bf16[2,512]{1,0:T(2,128)(2,1)S(1)} %pad_maximum_fusion.1, bf16[2048]{0:T(1024)(128)(2,1)S(1)} %copy-done.37), channel_id=1, replica_groups=mesh['dp'=16,'tensor'=2] {'dp'}, use_global_device_ids=true, to_apply=%region_21.22 | all-reduce | flops 3072 | bytes 12288 | tf_op jit(solution)/shard_map/psum | solution.py:240
  620.1 166.4 %all-reduce.4.cloned.1.call-done = (bf16[3,1024,512]{1,2,0:T(8,128)(2,1)}, bf16[512,1024]{1,0:T(8,128)(2,1)}, bf16[1024,2048]{1,0:T(8,128)(2,1)}, bf16[2048,1024]{1,0:T(8,128)(2,1)}) async-done(((bf16[3,1024,512]{1,2,0:T(8,128)(2,1)}, bf16[512,1024]{1,0:T(8,128)(2,1)}, bf16[1024,2048]{1,0:T(8,128)(2,1)}, bf16[2048,1024]{1,0:T(8,128)(2,1)}), (bf16[3,1024,512]{1,2,0:T(8,128)(2,1)}, ...) | async-done | bytes 12582928 | tf_op jit(solution)/shard_map/psum | solution.py:239
  794.7 6.8 convert_element_type.157
  (224 shorter events, 176.5 us)
Async XLA Ops:
  7.2 38.2 %copy-start = (bf16[3,1024,512]{2,1,0:T(8,128)(2,1)S(1)}, bf16[3,1024,512]{2,1,0:T(8,128)(2,1)}, u32[]{:S(2)}) copy-start(bf16[3,1024,512]{2,1,0:T(8,128)(2,1)} %param.18) | copy-start | bytes 9437188
  7.2 38.2 %all-gather.5.cloned.1.call-start = ((), (), s32[]{:S(2)}) async-start(), calls=%async_computation.4 | async-start | bytes 3145728 | tf_op jit(solution)/shard_map/all_gather | solution.py:131
  7.9 119.7 %reduce-scatter.5.cloned.1.call-start = ((), (), s32[]{:S(2)}) async-start(), calls=%async_computation.5 | async-start | bytes 3145728 | tf_op jit(solution)/shard_map/reduce_scatter | solution.py:151
  95.6 71.1 %all-gather.7.cloned.1.call-start = ((), (), s32[]{:S(2)}) async-start(), calls=%async_computation.6 | async-start | bytes 3145728 | tf_op jit(solution)/shard_map/all_gather | solution.py:161
  129.7 37.0 %copy-start.44 = (f32[2048]{0:T(1024)S(1)}, f32[2048]{0:T(1024)}, u32[]{:S(2)}) copy-start(f32[2048]{0:T(1024)} %param.25) | copy-start | bytes 24580
  133.5 98.3 %reduce-scatter.7.cloned.1.call-start = ((), (), s32[]{:S(2)}) async-start(), calls=%async_computation.7 | async-start | bytes 3145728 | tf_op jit(solution)/shard_map/reduce_scatter | solution.py:164
  166.8 27.3 %copy-start.38 = (bf16[2048,1024]{1,0:T(8,128)(2,1)S(1)}, bf16[2048,1024]{1,0:T(8,128)(2,1)}, u32[]{:S(2)}) copy-start(bf16[2048,1024]{1,0:T(8,128)(2,1)} %param.26) | copy-start | bytes 12582916
  199.7 72.8 %all-gather.9.cloned.1.call-start = ((), (), s32[]{:S(2)}) async-start(), calls=%async_computation.8 | async-start | bytes 3145728 | tf_op jit(solution)/shard_map/all_gather | solution.py:179
  239.3 84.5 %reduce-scatter.9.cloned.1.call-start = ((), (), s32[]{:S(2)}) async-start(), calls=%async_computation.9 | async-start | bytes 3145728 | tf_op jit(solution)/shard_map/reduce_scatter | solution.py:187
  272.5 13.5 %copy-start.39 = (bf16[1024,2048]{1,0:T(8,128)(2,1)S(1)}, bf16[1024,2048]{1,0:T(8,128)(2,1)}, u32[]{:S(2)}) copy-start(bf16[1024,2048]{1,0:T(8,128)(2,1)} %param.24) | copy-start | bytes 12582916
  291.8 74.0 %all-gather.11.cloned.1.call-start = ((), (), s32[]{:S(2)}) async-start(), calls=%async_computation.10 | async-start | bytes 3145728 | tf_op jit(solution)/shard_map/all_gather | solution.py:199
  332.5 284.4 %reduce-scatter.11.cloned.1.call-start = ((), (), s32[]{:S(2)}) async-start(), calls=%async_computation.11 | async-start | bytes 3145728 | tf_op jit(solution)/shard_map/reduce_scatter | solution.py:218
  332.6 38.4 %copy-start.27 = (f32[2,8,512]{2,1,0:T(8,128)S(1)}, f32[2,8,512]{2,1,0:T(8,128)}, u32[]{:S(2)}) copy-start(f32[2,8,512]{2,1,0:T(8,128)} %copy-done.26) | copy-start | bytes 98308
  374.8 9.7 %copy-start.3 = (bf16[1024,8,64]{0,2,1:T(8,128)(2,1)S(1)}, bf16[1024,8,64]{0,2,1:T(8,128)(2,1)}, u32[]{:S(2)}) copy-start(bf16[1024,8,64]{0,2,1:T(8,128)(2,1)} %get-tuple-element.460) | copy-start | bytes 3145732 | tf_op jit(solution)/shard_map/while
  374.8 9.7 %copy-start.7 = (bf16[1024,8,64]{0,2,1:T(8,128)(2,1)S(1)}, bf16[1024,8,64]{0,2,1:T(8,128)(2,1)}, u32[]{:S(2)}) copy-start(bf16[1024,8,64]{0,2,1:T(8,128)(2,1)} %get-tuple-element.458) | copy-start | bytes 3145732 | tf_op jit(solution)/shard_map/while
  397.0 18.4 %copy-start.1 = (f32[8,512,1024]{2,1,0:T(8,128)S(1)}, f32[8,512,1024]{2,1,0:T(8,128)}, u32[]{:S(2)}) copy-start(f32[8,512,1024]{2,1,0:T(8,128)} %get-tuple-element.383) | copy-start | bytes 50331652 | tf_op jit(solution)/shard_map/while
  397.0 18.6 %copy-start.12 = (bf16[1024,8,64]{0,2,1:T(8,128)(2,1)S(1)}, bf16[1024,8,64]{0,2,1:T(8,128)(2,1)}, u32[]{:S(2)}) copy-start(bf16[1024,8,64]{0,2,1:T(8,128)(2,1)} %get-tuple-element.462) | copy-start | bytes 3145732 | tf_op jit(solution)/shard_map/while
  432.4 9.7 %copy-start.3 = (bf16[1024,8,64]{0,2,1:T(8,128)(2,1)S(1)}, bf16[1024,8,64]{0,2,1:T(8,128)(2,1)}, u32[]{:S(2)}) copy-start(bf16[1024,8,64]{0,2,1:T(8,128)(2,1)} %get-tuple-element.460) | copy-start | bytes 3145732 | tf_op jit(solution)/shard_map/while
  432.4 9.7 %copy-start.7 = (bf16[1024,8,64]{0,2,1:T(8,128)(2,1)S(1)}, bf16[1024,8,64]{0,2,1:T(8,128)(2,1)}, u32[]{:S(2)}) copy-start(bf16[1024,8,64]{0,2,1:T(8,128)(2,1)} %get-tuple-element.458) | copy-start | bytes 3145732 | tf_op jit(solution)/shard_map/while
  454.6 18.4 %copy-start.1 = (f32[8,512,1024]{2,1,0:T(8,128)S(1)}, f32[8,512,1024]{2,1,0:T(8,128)}, u32[]{:S(2)}) copy-start(f32[8,512,1024]{2,1,0:T(8,128)} %get-tuple-element.383) | copy-start | bytes 50331652 | tf_op jit(solution)/shard_map/while
  454.6 18.6 %copy-start.12 = (bf16[1024,8,64]{0,2,1:T(8,128)(2,1)S(1)}, bf16[1024,8,64]{0,2,1:T(8,128)(2,1)}, u32[]{:S(2)}) copy-start(bf16[1024,8,64]{0,2,1:T(8,128)(2,1)} %get-tuple-element.462) | copy-start | bytes 3145732 | tf_op jit(solution)/shard_map/while
  512.3 274.2 %all-reduce.4.cloned.1.call-start = ((), (), s32[]{:S(2)}) async-start(), calls=%async_computation.12 | async-start | bytes 25165824 | tf_op jit(solution)/shard_map/psum | solution.py:239
  512.3 9.6 %copy-start.41 = (bf16[1024,1024]{1,0:T(8,128)(2,1)S(1)}, bf16[1024,1024]{1,0:T(8,128)(2,1)}, u32[]{:S(2)}) copy-start(bf16[1024,1024]{1,0:T(8,128)(2,1)} %all-gather.7.cloned.1.call-done) | copy-start | bytes 6291460
  535.9 44.7 %copy-start.37 = (bf16[2048]{0:T(1024)(128)(2,1)S(1)}, bf16[2048]{0:T(1024)(128)(2,1)}, u32[]{:S(2)}) copy-start(bf16[2048]{0:T(1024)(128)(2,1)} %get-tuple-element.257) | copy-start | bytes 12292
  (43 other events, 150.8 us)
Sparse Core Ops, SparseCore 0:
  9.6 35.7 all-gather.4
  95.8 31.8 reduce-scatter.4
  133.6 33.1 all-gather.6
  199.9 31.8 reduce-scatter.6
  239.4 33.1 all-gather.8
  291.9 31.8 reduce-scatter.8
  332.6 33.1 all-gather.10
  512.4 31.8 reduce-scatter.10
  550.0 236.4 all-reduce.3
where the time goes:
time: 822 us; the launch traced here: 813 us
  waiting for transfers between devices  398 us (48%)
  matrix products  179 us (22%)
  other arithmetic  88.8 us (11%)
  blocking collectives  75.8 us (9%)
  local copies, waits for them, and re-layouts  48.2 us (6%)
  between operations  14.6 us (2%)
    psum x1, waiting for transfers between devices, shards(): lax.psum(grad_qkv.astype(jnp.bfloat16), 'dp').astype(jnp.float32)  166 us
    psum x1, blocking collectives, shards(): shared = lax.psum(shared_terms, ('dp', 'tensor'))  40.8 us
    all_gather x1, waiting for transfers between devices, shards(): gathered = lax.all_gather(tokens, 'tensor', axis=0, tiled=True)  36.4 us
    psum x1, blocking collectives, shards(): lax.psum(grad_qv.astype(jnp.bfloat16), 'dp').astype(jnp.float32)  35.1 us
    dot_general x4, matrix products, masked_scores(): jnp.einsum('qhc,khc->hqk', query_rows, keys_all, preferred_element_type=j...  34.8 us
    all_gather x1, waiting for transfers between devices, shards(): lax.all_gather(second_grad.astype(jnp.bfloat16), 'tensor', axis=0, tiled=...  33.2 us
    all_gather x1, waiting for transfers between devices, shards(): lax.all_gather(normed.astype(jnp.bfloat16), 'tensor', axis=0, tiled=True)  33.2 us
    all_gather x1, waiting for transfers between devices, shards(): lax.all_gather(first_grad.astype(jnp.bfloat16), 'tensor', axis=0, tiled=T...  33.2 us
  transfers between devices with their start and end apart: 9, of which 8 were waited for; matrix products, arithmetic and copies ran while one was open for 4% of the time, Pallas kernels for 0%

commit v1 on v0

v1 whole, which is shorter than its diff:
```python
import functools
import math

import jax
import jax.numpy as jnp
from jax import lax
from jax.experimental import pallas as pl
from jax.experimental.pallas import tpu as pltpu
from jax.sharding import PartitionSpec as P

D = 1024
H = 16
DOCS_DEV = 4


EPSILON = 1e-06
ROOT_HALF = 0.7071067811865476
GAUSS_NORM = 0.3989422804014327
NT = (((1,), (1,)), ((), ()))
VMEM_ASK = 48 << 20


def norm_forward(summed, gain, shift):
    centred = summed - jnp.mean(summed, axis=-1, keepdims=True)
    inverse = lax.rsqrt(jnp.mean(centred * centred, axis=-1, keepdims=True) + EPSILON)
    unit = centred * inverse
    return (unit * gain + shift, unit, inverse)


def norm_backward(upstream, unit, inverse, gain):
    spread = upstream * gain
    inner = (
        spread
        - jnp.mean(spread, axis=-1, keepdims=True)
        - unit * jnp.mean(spread * unit, axis=-1, keepdims=True)
    )
    return (inner * inverse, jnp.sum(upstream * unit, axis=0), jnp.sum(upstream, axis=0))


def attn_forward_kernel(block, scale, own_ref, rest_ref, seen_ref, bar_ref, *refs):
    mixed_ref, lse_ref = refs[-2:]
    lane = lax.broadcasted_iota(jnp.int32, (1, 128), 1)
    rows = own_ref.shape[1] + rest_ref.shape[1]
    keys = jnp.concatenate([own_ref[1], rest_ref[1]], axis=0)
    values_t = jnp.concatenate([own_ref[2], rest_ref[2]], axis=0).T
    queries = jnp.concatenate([own_ref[0], rest_ref[0]], axis=0) * jnp.bfloat16(scale)
    half = [(lane // 64) == h for h in range(2)]
    keys_of = [jnp.where(half[h], keys, bar_ref[...]) for h in range(2)]
    for first in range(0, rows, block):
        span = slice(first, first + block)
        out_t = []
        for h in range(2):
            query = jnp.where(half[h], queries[span], seen_ref[span])
            scores = lax.dot_general(keys_of[h], query, NT, preferred_element_type=jnp.float32)
            top = jnp.max(scores, axis=0, keepdims=True)
            expd = jnp.exp(scores - top)
            total = jnp.sum(expd, axis=0, keepdims=True)
            mixed = jnp.dot(
                values_t[64 * h : 64 * h + 64],
                expd.astype(jnp.bfloat16),
                preferred_element_type=jnp.float32,
            )
            out_t.append(mixed / total)
            lse_ref[0, h : h + 1, span] = top + jnp.log(total)
        mixed_ref[span] = jnp.concatenate(out_t, axis=0).T.astype(jnp.bfloat16)


def attn_backward_kernel(
    block,
    scale,
    own_ref,
    rest_ref,
    up_own_ref,
    up_rest_ref,
    mixed_ref,
    lse_ref,
    seen_ref,
    bar_ref,
    *refs,
):
    grad_own_ref, grad_rest_ref, key_acc, value_acc = refs[-4:]
    lane = lax.broadcasted_iota(jnp.int32, (1, 128), 1)
    rows_own = own_ref.shape[1]
    rows = rows_own + rest_ref.shape[1]
    keys = jnp.concatenate([own_ref[1], rest_ref[1]], axis=0)
    values = jnp.concatenate([own_ref[2], rest_ref[2]], axis=0)
    keys_t = keys.T
    half = [(lane // 64) == h for h in range(2)]
    keys_of = [jnp.where(half[h], keys, bar_ref[...]) for h in range(2)]
    nothing = jnp.zeros((block, 128), jnp.bfloat16)
    for first in range(0, rows, block):
        span = slice(first, first + block)
        if first < rows_own:
            here, source, up_ref, out_ref = span, own_ref, up_own_ref, grad_own_ref
        else:
            here = slice(first - rows_own, first - rows_own + block)
            source, up_ref, out_ref = rest_ref, up_rest_ref, grad_rest_ref
        query_rows = source[0, here]
        up_rows = up_ref[here]
        product = (up_rows.astype(jnp.float32) * mixed_ref[span].astype(jnp.float32)).T
        query_grad_t = []
        for h in range(2):
            query = jnp.where(half[h], query_rows * jnp.bfloat16(scale), seen_ref[span])
            up = jnp.where(half[h], up_rows, nothing)
            scores = lax.dot_general(keys_of[h], query, NT, preferred_element_type=jnp.float32)
            probs = jnp.exp(scores - lse_ref[0, h : h + 1, span])
            spread = lax.dot_general(values, up, NT, preferred_element_type=jnp.float32)
            inner = jnp.sum(product[64 * h : 64 * h + 64], axis=0, keepdims=True)
            score_grad = (probs * (spread - inner)).astype(jnp.bfloat16)
            value_part = jnp.dot(probs.astype(jnp.bfloat16), up, preferred_element_type=jnp.float32)
            key_part = jnp.dot(
                score_grad, jnp.where(half[h], query_rows, nothing), preferred_element_type=jnp.float32
            )
            if first == 0 and h == 0:
                value_acc[...] = value_part
                key_acc[...] = key_part
            else:
                value_acc[...] += value_part
                key_acc[...] += key_part
            query_grad_t.append(
                jnp.dot(keys_t[64 * h : 64 * h + 64], score_grad, preferred_element_type=jnp.float32)
            )
        out_ref[0, here] = (jnp.concatenate(query_grad_t, axis=0).T * scale).astype(jnp.bfloat16)
    key_low = (key_acc[...] * scale).astype(jnp.bfloat16)
    value_low = value_acc[...].astype(jnp.bfloat16)
    grad_own_ref[1] = key_low[:rows_own]
    grad_rest_ref[1] = key_low[rows_own:]
    grad_own_ref[2] = value_low[:rows_own]
    grad_rest_ref[2] = value_low[rows_own:]


def attn_forward(own, rest, seen, bar, scale, block, start, count, previous=()):
    rows_own, rows_rest, width = own.shape[1], rest.shape[1], own.shape[2]
    rows = rows_own + rows_rest
    return pl.pallas_call(
        functools.partial(attn_forward_kernel, block, scale),
        grid=(count,),
        in_specs=[
            pl.BlockSpec((3, rows_own, 128), lambda p: (0, 0, p + start)),
            pl.BlockSpec((3, rows_rest, 128), lambda p: (0, 0, p + start)),
            pl.BlockSpec((rows, 128), lambda p: (0, 0)),
            pl.BlockSpec((rows, 128), lambda p: (0, 0)),
        ]
        + [pl.BlockSpec(memory_space=pl.ANY)] * len(previous),
        out_specs=[
            pl.BlockSpec((rows, 128), lambda p: (0, p + start)),
            pl.BlockSpec((1, 8, rows), lambda p: (p + start, 0, 0)),
        ],
        out_shape=[
            jax.ShapeDtypeStruct((rows, width), jnp.bfloat16),
            jax.ShapeDtypeStruct((width // 128, 8, rows), jnp.float32),
        ],
        input_output_aliases={4: 0, 5: 1} if previous else {},
        compiler_params=pltpu.CompilerParams(vmem_limit_bytes=VMEM_ASK),
        cost_estimate=pl.CostEstimate(
            flops=count * 16 * 256 * rows * rows,
            transcendentals=count * 2 * rows * rows,
            bytes_accessed=count * 10 * 128 * rows,
        ),
        name="attn_forward",
    )(own, rest, seen, bar, *previous)


def attn_backward(
    own, rest, up_own, up_rest, mixed, lse, seen, bar, scale, block, start, count, previous=()
):
    rows_own, rows_rest, width = own.shape[1], rest.shape[1], own.shape[2]
    rows = rows_own + rows_rest
    return pl.pallas_call(
        functools.partial(attn_backward_kernel, block, scale),
        grid=(count,),
        in_specs=[
            pl.BlockSpec((3, rows_own, 128), lambda p: (0, 0, p + start)),
            pl.BlockSpec((3, rows_rest, 128), lambda p: (0, 0, p + start)),
            pl.BlockSpec((rows_own, 128), lambda p: (0, p + start)),
            pl.BlockSpec((rows_rest, 128), lambda p: (0, p + start)),
            pl.BlockSpec((rows, 128), lambda p: (0, p + start)),
            pl.BlockSpec((1, 8, rows), lambda p: (p + start, 0, 0)),
            pl.BlockSpec((rows, 128), lambda p: (0, 0)),
            pl.BlockSpec((rows, 128), lambda p: (0, 0)),
        ]
        + [pl.BlockSpec(memory_space=pl.ANY)] * len(previous),
        out_specs=[
            pl.BlockSpec((3, rows_own, 128), lambda p: (0, 0, p + start)),
            pl.BlockSpec((3, rows_rest, 128), lambda p: (0, 0, p + start)),
        ],
        out_shape=[
            jax.ShapeDtypeStruct((3, rows_own, width), jnp.bfloat16),
            jax.ShapeDtypeStruct((3, rows_rest, width), jnp.bfloat16),
        ],
        input_output_aliases={8: 0, 9: 1} if previous else {},
        scratch_shapes=[pltpu.VMEM((rows, 128), jnp.float32)] * 2,
        compiler_params=pltpu.CompilerParams(vmem_limit_bytes=VMEM_ASK),
        cost_estimate=pl.CostEstimate(
            flops=count * 24 * 256 * rows * rows,
            transcendentals=count * 2 * rows * rows,
            bytes_accessed=count * 18 * 128 * rows,
        ),
        name="attn_backward",
    )(own, rest, up_own, up_rest, mixed, lse, seen, bar, *previous)


def doc_features(docs):
    slot = lax.broadcasted_iota(jnp.int32, (1, 128), 1) % 64
    same = docs[:, None] == slot
    seen = same.astype(jnp.bfloat16)
    bar = jnp.where(same | (slot > 4), 0.0, -(2.0**30)).astype(jnp.bfloat16)
    return seen, bar


def xor_step(array, mask):
    size = lax.axis_size("dp")
    return lax.ppermute(array, "dp", [(i, i ^ mask) for i in range(size)])


def from_rank(array, ahead):
    size = lax.axis_size("tensor")
    return lax.ppermute(array, "tensor", [((i + ahead) % size, i) for i in range(size)])


def exchange(parts):
    size = lax.axis_size("tensor")
    got = [None] * size
    for ahead in range(1, size):
        got[size - ahead] = lax.ppermute(
            parts[ahead], "tensor", [(i, (i + ahead) % size) for i in range(size)]
        )
    return got


def meet(*trees):
    return lax.optimization_barrier(trees)


def spread_kernel(count, order_ref, near_ref, far_ref, out_ref):
    step = pl.program_id(0)
    rows = near_ref.shape[0] // count

    def store(ref):
        for index in range(count):
            offset = pl.multiple_of(order_ref[4 + index] * rows, rows)
            out_ref[pl.ds(offset, rows)] = ref[index * rows : (index + 1) * rows].astype(
                out_ref.dtype
            )

    @pl.when(step < 2)
    def _():
        store(near_ref)

    @pl.when(step > 1)
    def _():
        store(far_ref)


def spread(near, far, place, count, kind):
    rows, columns = near.shape[0] // 2, near.shape[1]
    quarter, inner = lax.div(place, jnp.int32(count)), lax.rem(place, jnp.int32(count))
    order = jnp.concatenate(
        [
            jnp.bitwise_xor(quarter, jnp.arange(4, dtype=jnp.int32)),
            jnp.bitwise_xor(inner, jnp.arange(count, dtype=jnp.int32)),
        ]
    )
    return pl.pallas_call(
        functools.partial(spread_kernel, count),
        grid_spec=pltpu.PrefetchScalarGridSpec(
            num_scalar_prefetch=1,
            grid=(4,),
            in_specs=[
                pl.BlockSpec((rows, columns), lambda step, order: (jnp.minimum(step, 1), 0)),
                pl.BlockSpec((rows, columns), lambda step, order: (jnp.maximum(step - 2, 0), 0)),
            ],
            out_specs=pl.BlockSpec((rows, columns), lambda step, order: (order[step], 0)),
        ),
        out_shape=jax.ShapeDtypeStruct((4 * rows, columns), kind),
        compiler_params=pltpu.CompilerParams(vmem_limit_bytes=VMEM_ASK // 2),
        cost_estimate=pl.CostEstimate(
            flops=0, transcendentals=0, bytes_accessed=24 * rows * columns
        ),
        name="spread_rows",
    )(order, near, far)


def bit_of(dp_pos, mask):
    return jnp.where(lax.bitwise_and(dp_pos, mask) != 0, 1, 0).astype(jnp.int32)


def half_of(array, index):
    rows = array.shape[0] // 2
    return lax.dynamic_slice_in_dim(array, index * rows, rows, 0)


def opening(parts, dp_pos, mask):
    bit = bit_of(dp_pos, mask)
    return [half_of(part, 1 - bit) for part in parts], [half_of(part, bit) for part in parts]


def send(arrays, mask):
    return [xor_step(array, mask) for array in arrays]


def add(keep, got):
    return [
        (a.astype(jnp.float32) + b.astype(jnp.float32)).astype(a.dtype)
        for a, b in zip(keep, got, strict=True)
    ]


def fold(keep, got, dp_pos, mask):
    bit = bit_of(dp_pos, mask)
    away = add([half_of(a, 1 - bit) for a in keep], [half_of(b, 1 - bit) for b in got])
    kept = add([half_of(a, bit) for a in keep], [half_of(b, bit) for b in got])
    return away, kept


def fold_ranks(keep, got):
    total = add(keep, got)
    return [total[0]], exchange(total)[1:]


def add_ranks(keep, got):
    total = keep[0].astype(jnp.float32)
    for piece in got:
        total = total + piece.astype(jnp.float32)
    return total.astype(keep[0].dtype)


def scatter_on(array, dp_pos, masks):
    for mask in masks:
        away, keep = opening([array], dp_pos, mask)
        array = add(keep, send(away, mask))[0]
    return array


def gather_rows(mine, dp_pos, masks):
    for mask in reversed(masks[1:]):
        mine = jnp.concatenate([mine, xor_step(mine, mask)], axis=0)
    place = jnp.int32(0)
    for mask in masks:
        place = 2 * place + bit_of(dp_pos, mask)
    return spread(mine, xor_step(mine, masks[0]), place, 2 ** (len(masks) - 2), jnp.float32)


def butterfly(array, axis):
    size = lax.axis_size(axis)
    mask = 1
    while mask < size:
        array = array + lax.ppermute(array, axis, [(i, i ^ mask) for i in range(size)])
        mask *= 2
    return array


def shards(
    tokens,
    doc_ids,
    w_qkv,
    qv_bias,
    out_weight,
    out_biases,
    ln_gains,
    ln_shifts,
    up_weight,
    up_bias,
    down_weight,
    cotangent,
):
    low = jnp.bfloat16
    rows_own = tokens.shape[0]
    ranks = lax.axis_size("tensor")
    tensor_pos = lax.axis_index("tensor")
    dp_pos = lax.axis_index("dp")
    head_size = D // H
    width = w_qkv.shape[2]
    scale = 1.0 / math.sqrt(head_size)

    count_dp = lax.axis_size("dp")
    masks = [2**k for k in range(count_dp.bit_length() - 1)]
    masks_up = [masks[0], masks[2], masks[1]] + masks[3:]
    others = range(1, ranks)

    rest = [from_rank(tokens, ahead) for ahead in others]
    rest = rest[0] if ranks == 2 else jnp.concatenate(rest, axis=0)
    up_biases = [up_bias] + [from_rank(up_bias, ahead) for ahead in others]
    out_own, up_own, down_own, rest = meet(out_weight, up_weight, down_weight, rest)

    place = 4 * bit_of(dp_pos, 1) + 2 * bit_of(dp_pos, 4) + bit_of(dp_pos, 2)

    def slice_from(weight, pieces, index):
        rows = weight.shape[0] // pieces
        mine = lax.dynamic_slice_in_dim(weight, index * rows, rows, 0)
        return [from_rank(mine, ahead) for ahead in others]

    def joined(groups):
        return [jnp.concatenate(items, axis=0) for items in zip(*groups, strict=True)]

    def corner(by_first, by_second):
        rows = by_first[0].shape[0] // 2
        return (
            [xor_step(item[:rows], 2) for item in by_second],
            [xor_step(item[rows:], 4) for item in by_first],
        )

    out_place = 2 * bit_of(dp_pos, 1) + bit_of(dp_pos, 2)
    out_first, up_first, down_first = (
        slice_from(out_own, 4, out_place),
        slice_from(up_own, 8, place),
        slice_from(down_own, 8, place),
    )
    docs = [
        lax.dynamic_slice_in_dim(
            doc_ids, lax.rem(tensor_pos + ahead, ranks) * rows_own, rows_own, 0
        )
        for ahead in range(ranks)
    ]
    seen, bar = doc_features(jnp.concatenate(docs, axis=0))
    bias = jnp.stack([qv_bias[0], jnp.zeros_like(qv_bias[0]), qv_bias[1]])[:, None, :]

    def project(rows):
        wide = jnp.einsum("sd,idc->isc", rows, w_qkv, preferred_element_type=jnp.float32)
        return (wide + bias).astype(low)

    qkv_own, qkv_rest = project(tokens), project(rest)
    pairs = width // 128
    early = max(1, pairs // 2)
    block = min(512, rows_own)
    mixed_lse = attn_forward(qkv_own, qkv_rest, seen, bar, scale, block, 0, early)
    mixed_lse, out_first, up_first = meet(mixed_lse, out_first, up_first)
    out_second = send(out_first, 2)
    up_second, up_third = send(up_first, 2), send(up_first, 4)
    if pairs > early:
        mixed_lse = attn_forward(
            qkv_own, qkv_rest, seen, bar, scale, block, early, pairs - early, tuple(mixed_lse)
        )
    mixed_lse, out_second, down_first = meet(mixed_lse, out_second, down_first)
    out_half = joined([out_first, out_second])
    out_far = send(out_half, 1)
    down_second, down_third = send(down_first, 2), send(down_first, 4)
    mixed, lse = mixed_lse
    mixed_parts = [mixed[k * rows_own : (k + 1) * rows_own] for k in range(ranks)]
    mixed_got = exchange(mixed_parts)
    mixed_got[0] = mixed_parts[0]
    mixed_got, out_far, up_second, up_third = meet(mixed_got, out_far, up_second, up_third)
    up_corner = corner(up_second, up_third)
    outs = [out_own] + [
        spread(near, far, out_place, 1, low) for near, far in zip(out_half, out_far, strict=True)
    ]
    attention = sum(
        jnp.dot(mixed_got[k], outs[k], preferred_element_type=jnp.float32) for k in range(ranks)
    )
    inputs_own = tokens.astype(jnp.float32)
    normed, unit_first, inverse_first = norm_forward(
        inputs_own + attention + out_biases[0], ln_gains[0], ln_shifts[0]
    )
    normed_low = normed.astype(low)

    def activate(up, up_bias):
        hidden = jnp.dot(normed_low, up, preferred_element_type=jnp.float32) + up_bias
        below = 0.5 * (1.0 + lax.erf(hidden * ROOT_HALF))
        density = jnp.exp(-0.5 * hidden * hidden) * GAUSS_NORM
        return meet((hidden * below).astype(low), (below + hidden * density).astype(low))

    normed_low, up_corner, down_second, down_third = meet(
        normed_low, up_corner, down_second, down_third
    )
    up_half = joined([up_first, up_second, up_third, *up_corner])
    up_far = send(up_half, 1)
    down_corner = corner(down_second, down_third)
    pairs_active = [activate(up_own, up_bias)]
    pairs_active, up_far = meet(pairs_active, up_far)
    ups = [up_own] + [
        spread(near, far, place, 2, low) for near, far in zip(up_half, up_far, strict=True)
    ]
    ups, down_corner = meet(ups, down_corner)
    down_half = joined([down_first, down_second, down_third, *down_corner])
    down_far = send(down_half, 1)
    pairs_active += [activate(ups[k], up_biases[k]) for k in others]
    pairs_active, down_far = meet(pairs_active, down_far)
    downs = [down_own] + [
        spread(near, far, place, 2, low) for near, far in zip(down_half, down_far, strict=True)
    ]
    active, slope = zip(*pairs_active, strict=True)
    branch = 0.0
    for k in range(ranks):
        branch = branch + jnp.dot(active[k], downs[k], preferred_element_type=jnp.float32)
    result, unit_second, inverse_second = norm_forward(
        normed + branch + out_biases[1], ln_gains[1], ln_shifts[1]
    )

    out_grad = cotangent.astype(jnp.float32) * (docs[0] < DOCS_DEV).astype(jnp.float32)[:, None]
    second_grad, gain_grad_second, shift_grad_second = norm_backward(
        out_grad, unit_second, inverse_second, ln_gains[1]
    )
    bias_grad_second = jnp.sum(second_grad, axis=0)
    branch_grad = second_grad.astype(low)
    down_parts = [
        jnp.einsum("sf,sd->fd", active[k], branch_grad, preferred_element_type=jnp.float32).astype(
            low
        )
        for k in range(ranks)
    ]
    down_parts, branch_grad = meet(down_parts, branch_grad)
    down_away, down_keep = opening(down_parts, dp_pos, masks[0])
    down_away, branch_grad = meet(down_away, branch_grad)
    down_got = send(down_away, masks[0])
    hidden_grads = []
    for k in range(ranks):
        active_grad = jnp.einsum(
            "sd,fd->sf", branch_grad, downs[k], preferred_element_type=jnp.float32
        )
        hidden_grads.append((active_grad * slope[k].astype(jnp.float32)).astype(low))
    hidden_grads, down_got = meet(hidden_grads, down_got)
    down_away, down_keep = fold(down_keep, down_got, dp_pos, masks[1])
    down_away, hidden_grads = meet(down_away, hidden_grads)
    down_got = send(down_away, masks[1])
    up_parts = [
        jnp.einsum(
            "sd,sf->df", normed_low, hidden_grads[k], preferred_element_type=jnp.float32
        ).astype(low)
        for k in range(ranks)
    ]
    up_away, up_keep = opening(up_parts, dp_pos, masks_up[0])
    up_away, hidden_grads = meet(up_away, hidden_grads)
    up_got = send(up_away, masks_up[0])
    normed_grad = second_grad
    for k in range(ranks):
        normed_grad = normed_grad + jnp.einsum(
            "sf,df->sd", hidden_grads[k], ups[k], preferred_element_type=jnp.float32
        )
    first_grad, gain_grad_first, shift_grad_first = norm_backward(
        normed_grad, unit_first, inverse_first, ln_gains[0]
    )
    bias_grad_first = jnp.sum(first_grad, axis=0)
    attn_grad = first_grad.astype(low)
    mixed_grads = [
        jnp.einsum("sd,cd->sc", attn_grad, outs[k], preferred_element_type=jnp.float32).astype(low)
        for k in range(ranks)
    ]
    mixed_grads, up_got = meet(mixed_grads, up_got)
    grads_got = exchange(mixed_grads)
    up_away, up_keep = fold(up_keep, up_got, dp_pos, masks_up[1])
    up_got = send(up_away, masks_up[1])
    out_parts = [
        jnp.einsum("sc,sd->cd", mixed_got[k], attn_grad, preferred_element_type=jnp.float32).astype(
            low
        )
        for k in range(ranks)
    ]
    out_away, out_keep = opening(out_parts, dp_pos, masks[0])
    out_away, grads_got = meet(out_away, grads_got[1:])
    out_got = send(out_away, masks[0])
    grads_rest = grads_got[0] if ranks == 2 else jnp.concatenate(grads_got, axis=0)
    block = min(256, rows_own)
    qkv_grads = attn_backward(
        qkv_own, qkv_rest, mixed_grads[0], grads_rest, mixed, lse, seen, bar, scale, block, 0, early
    )
    qkv_grads, down_got, out_got = meet(qkv_grads, down_got, out_got)
    down_keep, down_got = fold_ranks(down_keep, down_got)
    out_away, out_keep = fold(out_keep, out_got, dp_pos, masks[1])
    out_got = send(out_away, masks[1])
    if pairs > early:
        qkv_grads = attn_backward(
            qkv_own,
            qkv_rest,
            mixed_grads[0],
            grads_rest,
            mixed,
            lse,
            seen,
            bar,
            scale,
            block,
            early,
            pairs - early,
            tuple(qkv_grads),
        )
    qkv_grads, down_got, up_got, out_got = meet(qkv_grads, down_got, up_got, out_got)
    down_sum = add_ranks(down_keep, down_got)
    down_away, down_keep = opening([down_sum], dp_pos, masks[2])
    down_got = send(down_away, masks[2])
    up_keep, up_got = fold_ranks(up_keep, up_got)
    out_keep, out_got = fold_ranks(out_keep, out_got)
    qkv_grad_own, qkv_grad_rest = qkv_grads

    def input_part(item):
        return jnp.einsum("isc,idc->sd", item, w_qkv, preferred_element_type=jnp.float32)

    grad_qkv = jnp.einsum("sd,isc->idc", rest, qkv_grad_rest, preferred_element_type=jnp.float32)
    grad_qkv = grad_qkv + jnp.einsum(
        "sd,isc->idc", tokens, qkv_grad_own, preferred_element_type=jnp.float32
    )
    qkv_away, qkv_keep = opening([grad_qkv.astype(low).reshape(3 * D, width)], dp_pos, masks[0])
    qkv_got = send(qkv_away, masks[0])
    far = input_part(qkv_grad_rest).astype(low)
    far, qkv_got, down_got = meet(far, qkv_got, down_got)
    qkv_away, qkv_keep = fold(qkv_keep, qkv_got, dp_pos, masks[1])
    qkv_got = send(qkv_away, masks[1])
    down_sum = scatter_on(add(down_keep, down_got)[0], dp_pos, masks[3:])
    near = input_part(qkv_grad_own)
    near, up_got, far = meet(near, up_got, far)
    inputs_got = exchange(
        [None] + [far[k * rows_own : (k + 1) * rows_own] for k in range(ranks - 1)]
    )
    up_sum = scatter_on(add_ranks(up_keep, up_got), dp_pos, masks_up[2:])
    qkv_sum = scatter_on(add(qkv_keep, qkv_got)[0], dp_pos, masks[2:])
    grad_down = gather_rows(down_sum, dp_pos, masks)
    grad_up = gather_rows(up_sum, dp_pos, masks_up)
    grad_qkv = gather_rows(qkv_sum, dp_pos, masks)
    out_sum = add_ranks(out_keep, out_got)
    if (out_sum.shape[0] * 4 // count_dp) % 16 == 0:
        grad_out = gather_rows(scatter_on(out_sum, dp_pos, masks[2:]), dp_pos, masks)
    else:
        for mask in masks[2:]:
            out_sum = add([out_sum], send([out_sum], mask))[0]
        half = jnp.concatenate([out_sum, xor_step(out_sum, masks[1])], axis=0)
        grad_out = spread(half, xor_step(half, masks[0]), out_place, 1, jnp.float32)

    up_sums = [jnp.sum(item.astype(jnp.float32), axis=0) for item in hidden_grads]
    sums_got = exchange(up_sums)
    hidden_sum = up_sums[0]
    for piece in sums_got[1:]:
        hidden_sum = hidden_sum + piece
    shared = butterfly(
        jnp.stack(
            [
                bias_grad_first,
                bias_grad_second,
                gain_grad_first,
                gain_grad_second,
                shift_grad_first,
                shift_grad_second,
            ]
        ),
        "tensor",
    )
    shared = butterfly(jnp.concatenate([shared.reshape(-1), hidden_sum]), "dp")
    shared, grad_up_bias = shared[: 6 * D].reshape(6, D), shared[6 * D :]
    qkv_sums = jnp.sum(qkv_grad_own.astype(jnp.float32), axis=1) + jnp.sum(
        qkv_grad_rest.astype(jnp.float32), axis=1
    )
    grad_qv = butterfly(jnp.stack([qkv_sums[0], qkv_sums[2]]), "dp")
    grad_input = first_grad + near
    for piece in inputs_got[1:]:
        grad_input = grad_input + piece.astype(jnp.float32)
    return (
        result.astype(low),
        grad_input.astype(low),
        grad_qkv.reshape(3, D, width),
        grad_qv,
        grad_out,
        shared[0:2],
        shared[2:4],
        shared[4:6],
        grad_up,
        grad_up_bias,
        grad_down,
    )


def solution(mesh):
    placed = (
        P(("dp", "tensor"), None),
        P("dp"),
        P(None, None, "tensor"),
        P(None, "tensor"),
        P("tensor", None),
        P(),
        P(),
        P(),
        P(None, "tensor"),
        P("tensor"),
        P("tensor", None),
        P(("dp", "tensor"), None),
    )
    return jax.shard_map(
        shards,
        mesh=mesh,
        in_specs=placed,
        out_specs=(
            P(("dp", "tensor"), None),
            P(("dp", "tensor"), None),
            P(None, None, "tensor"),
            P(None, "tensor"),
            P("tensor", None),
            P(),
            P(),
            P(),
            P(None, "tensor"),
            P("tensor"),
            P("tensor", None),
        ),
        check_vma=False,
    )
```

time: 822 us -> 512 us (0.62)
  waiting for transfers between devices: 398 us -> 177 us
  matrix products: 179 us -> 72.9 us
  blocking collectives: 75.8 us -> 0 us
  Pallas kernels: 0 us -> 73.9 us
  starting transfers between devices: 0.99 us -> 70.6 us
  other arithmetic: 88.8 us -> 58.7 us
  between operations: 14.6 us -> 2.12 us
    ppermute x0 -> x71, waiting for transfers between devices: none -> 177 us  [the longest x50 142 us: xor_step(): return lax.ppermute(array, 'dp', [(i, i ^ mask) for i in range(size)])]
    psum x1 -> x0, waiting for transfers between devices: 166 us -> none  [shards(): lax.psum(grad_qkv.astype(jnp.bfloat16), 'dp').astype(jnp.float32)]
    all_gather x4 -> x0, waiting for transfers between devices: 136 us -> none  [the longest x1 36.4 us: shards(): gathered = lax.all_gather(tokens, 'tensor', axis=0, tiled=True)]
    dot_general x26 -> x24, matrix products: 179 us -> 72.9 us  [the longest x2 14.6 us: activate(): jnp.dot(normed_low, up, preferred_element_type=jnp.float32) + up_bias]
    reduce_scatter x4 -> x0, waiting for transfers between devices: 95 us -> none  [the longest x1 31.9 us: shards(): lax.psum_scatter(jnp.einsum('sf,df->sd', hidden_low, up_weight, preferred...]
    psum x2 -> x0, blocking collectives: 75.8 us -> none  [the longest x1 40.8 us: shards(): shared = lax.psum(shared_terms, ('dp', 'tensor'))]
    pallas_call x0 -> x11, Pallas kernels: none -> 73.9 us  [the longest x7 32.3 us: spread(): pl.pallas_call(functools.partial(spread_kernel, count), grid_spec=pltpu.P...]
    ppermute x0 -> x71, starting transfers between devices: none -> 70.6 us  [the longest x50 45.4 us: xor_step(): return lax.ppermute(array, 'dp', [(i, i ^ mask) for i in range(size)])]
  transfers between devices with their start and end apart: 9 -> 71, of which waited for: 8 -> 27; matrix products, arithmetic and copies ran while one was open for 4% -> 25% of each run, Pallas kernels for 0% -> 12%
where the time goes in v1:
time: 512 us; the launch traced here: 507 us
  waiting for transfers between devices  177 us (35%)
  Pallas kernels  73.9 us (14%)
  matrix products  72.9 us (14%)
  starting transfers between devices  70.6 us (14%)
  other arithmetic  58.7 us (11%)
  local copies, waits for them, and re-layouts  51.9 us (10%)
    ppermute x50, waiting for transfers between devices, xor_step(): return lax.ppermute(array, 'dp', [(i, i ^ mask) for i in range(size)])  142 us
    ppermute x50, starting transfers between devices, xor_step(): return lax.ppermute(array, 'dp', [(i, i ^ mask) for i in range(size)])  45.4 us
    pallas_call x7, Pallas kernels, spread(): pl.pallas_call(functools.partial(spread_kernel, count), grid_spec=pltpu.P...  32.3 us
    pallas_call x2, Pallas kernels, attn_backward(): pl.pallas_call(functools.partial(attn_backward_kernel, block, scale), gri...  24.3 us
    convert_element_type x19, other arithmetic, add(): (a.astype(jnp.float32) + b.astype(jnp.float32)).astype(a.dtype)  23.6 us
    ppermute x5, waiting for transfers between devices, from_rank(): lax.ppermute(array, 'tensor', [((i + ahead) % size, i) for i in range(siz...  23.1 us
    unnamed x155, local copies, waits for them, and re-layouts  22.1 us
    pallas_call x2, Pallas kernels, attn_forward(): pl.pallas_call(functools.partial(attn_forward_kernel, block, scale), grid...  17.3 us
  transfers between devices with their start and end apart: 71, of which 27 were waited for; matrix products, arithmetic and copies ran while one was open for 25% of the time, Pallas kernels for 12%

profile of v1, /device:TPU:0, one launch (start us, length us, event | category | flops | bytes accessed | tf_op | source)
XLA Modules:
  0.0 507.5 jit_solution(12536523260522057842)
XLA Ops:
  13.0 14.1 %collective-permute-done = bf16[512,1024]{1,0:T(8,128)(2,1)} collective-permute-done((bf16[512,1024]{1,0:T(8,128)(2,1)}, bf16[512,1024]{1,0:T(8,128)(2,1)}, u32[]{:S(2)}, u32[]{:S(2)}) %collective-permute-start) | collective-permute-done | bytes 1048608 | tf_op jit(solution)/shard_map/ppermute | solution.py:218
  36.3 8.8 %attn_forward.2 = (bf16[1024,512]{1,0:T(8,128)(2,1)S(1)}, f32[4,8,1024]{2,1,0:T(8,128)S(1)}) custom-call(bf16[3,512,512]{2,1,0:T(8,128)(2,1)S(1)} %fusion.15.own_ref, bf16[3,512,512]{2,1,0:T(8,128)(2,1)S(1)} %fusion.16.rest_ref, bf16[1024,128]{1,0:T(8,128)(2,1)S(1)} %compare_convert_fusion.seen_ref, bf16[1024,128]{1,0:T(8,128)(2,1)S(1)} %select_convert_fusion.bar_ref), custom_call_target="tpu_custom_call" | custom-call | flops 8589934592 | bytes 2621440 | tf_op jit(solution)/shard_map/attn_forward/pallas_call | solution.py:135
  45.2 5.6 %collective-permute-done.2 = bf16[128,2048]{1,0:T(8,128)(2,1)S(1)} collective-permute-done((bf16[128,2048]{1,0:T(8,128)(2,1)S(1)}, bf16[128,2048]{1,0:T(8,128)(2,1)S(1)}, u32[]{:S(2)}, u32[]{:S(2)}) %collective-permute-start.2) | collective-permute-done | bytes 524320 | tf_op jit(solution)/shard_map/ppermute | solution.py:218
  54.6 8.4 %attn_forward.3 = (bf16[1024,512]{1,0:T(8,128)(2,1)S(1)}, f32[4,8,1024]{2,1,0:T(8,128)S(1)}) custom-call(bf16[3,512,512]{2,1,0:T(8,128)(2,1)S(1)} %fusion.15.own_ref, bf16[3,512,512]{2,1,0:T(8,128)(2,1)S(1)} %fusion.16.rest_ref, bf16[1024,128]{1,0:T(8,128)(2,1)S(1)} %compare_convert_fusion.seen_ref, ...), custom_call_target="tpu_custom_call", output_to_operand_aliasing={{0}: (4, {}), {1}: (5, {})} | custom-call | flops 8589934592 | bytes 2621440 | tf_op jit(solution)/shard_map/attn_forward/pallas_call | solution.py:135
  97.9 7.8 %fusion.4 = (bf16[512,2048]{1,0:T(8,128)(2,1)}, bf16[512,2048]{1,0:T(8,128)(2,1)}) fusion(f32[2048]{0:T(1024)} %param.21, bf16[512,1024]{1,0:T(8,128)(2,1)S(1)} %copy-done.40, bf16[1024,2048]{1,0:T(8,128)(2,1)} %param.20), kind=kOutput, calls=%fused_computation.7 | convolution fusion | flops 2160066560 | bytes 9445376 | tf_op jit(solution)/shard_map/dot_general | solution.py:457
  120.8 6.8 %fusion.9 = (bf16[512,2048]{1,0:T(8,128)(2,1)}, bf16[512,2048]{1,0:T(8,128)(2,1)S(1)}) fusion(f32[2048]{0:T(1024)} %collective-permute-done.16, bf16[512,1024]{1,0:T(8,128)(2,1)} %fusion.14, bf16[1024,2048]{1,0:T(8,128)(2,1)} %copy-done.3), kind=kOutput, calls=%fused_computation.12 | convolution fusion | flops 2160066560 | bytes 9445376 | tf_op jit(solution)/shard_map/dot_general | solution.py:457
  155.8 5.7 %multiply_convert_fusion.1 = bf16[512,2048]{1,0:T(8,128)(2,1)S(1)} fusion(bf16[512,2048]{1,0:T(8,128)(2,1)} %get-tuple-element.143, bf16[512,1024]{1,0:T(8,128)(2,1)} %copy-done.37, bf16[2048,1024]{1,0:T(8,128)(2,1)} %param.22), kind=kOutput, calls=%fused_computation.16 | convolution fusion | flops 2150629376 | bytes 9437184 | tf_op jit(solution)/shard_map/sd,fd->sf/dot_general | solution.py:507
  226.1 12.1 %attn_backward.2 = (bf16[3,512,512]{2,1,0:T(8,128)(2,1)S(1)}, bf16[3,512,512]{2,1,0:T(8,128)(2,1)S(1)}) custom-call(bf16[3,512,512]{2,1,0:T(8,128)(2,1)} %copy-done.16, bf16[3,512,512]{2,1,0:T(8,128)(2,1)} %copy-done.17, bf16[512,512]{1,0:T(8,128)(2,1)S(1)} %copy-done.15, bf16[512,512]{1,0:T(8,128)(2,1)S(1)} %collective-permute-done.22.up_rest_ref, ...), custom_call_target="tpu_custom_call" | custom-call | flops 12884901888 | bytes 4718592 | tf_op jit(solution)/shard_map/attn_backward/pallas_call | solution.py:169
  242.1 18.7 %collective-permute-done.24 = bf16[512,1024]{1,0:T(8,128)(2,1)S(1)} collective-permute-done((bf16[512,1024]{1,0:T(8,128)(2,1)S(1)}, bf16[512,1024]{1,0:T(8,128)(2,1)S(1)}, u32[]{:S(2)}, u32[]{:S(2)}) %collective-permute-start.24) | collective-permute-done | bytes 1048608 | tf_op jit(solution)/shard_map/ppermute | solution.py:213
  269.9 12.3 %attn_backward.3 = (bf16[3,512,512]{2,1,0:T(8,128)(2,1)S(1)}, bf16[3,512,512]{2,1,0:T(8,128)(2,1)S(1)}) custom-call(bf16[3,512,512]{2,1,0:T(8,128)(2,1)} %copy-done.16, bf16[3,512,512]{2,1,0:T(8,128)(2,1)} %copy-done.17, bf16[512,512]{1,0:T(8,128)(2,1)S(1)} %copy-done.15, ...), custom_call_target="tpu_custom_call", output_to_operand_aliasing={{0}: (8, {}), {1}: (9, {})} | custom-call | flops 12884901888 | bytes 4718592 | tf_op jit(solution)/shard_map/attn_backward/pallas_call | solution.py:169
  292.1 4.7 fusion.10
  296.8 4.9 copy.31
  329.1 10.5 %collective-permute-done.66 = bf16[128,1024]{1,0:T(8,128)(2,1)S(1)} collective-permute-done((bf16[128,1024]{1,0:T(8,128)(2,1)S(1)}, bf16[128,1024]{1,0:T(8,128)(2,1)S(1)}, u32[]{:S(2)}, u32[]{:S(2)}) %collective-permute-start.66) | collective-permute-done | bytes 262176 | tf_op jit(solution)/shard_map/ppermute | solution.py:213
  342.9 11.1 %collective-permute-done.36 = bf16[768,512]{1,0:T(8,128)(2,1)S(1)} collective-permute-done((bf16[768,512]{1,0:T(8,128)(2,1)S(1)}, bf16[768,512]{1,0:T(8,128)(2,1)S(1)}, u32[]{:S(2)}, u32[]{:S(2)}) %collective-permute-start.36) | collective-permute-done | bytes 786464 | tf_op jit(solution)/shard_map/ppermute | solution.py:213
  356.1 8.6 %collective-permute-done.61 = bf16[64,2048]{1,0:T(8,128)(2,1)S(1)} collective-permute-done((bf16[64,2048]{1,0:T(8,128)(2,1)S(1)}, bf16[64,2048]{1,0:T(8,128)(2,1)S(1)}, u32[]{:S(2)}, u32[]{:S(2)}) %collective-permute-start.61) | collective-permute-done | bytes 262176 | tf_op jit(solution)/shard_map/ppermute | solution.py:213
  368.0 9.6 %collective-permute-done.62 = bf16[64,2048]{1,0:T(8,128)(2,1)S(1)} collective-permute-done((bf16[64,2048]{1,0:T(8,128)(2,1)S(1)}, bf16[64,2048]{1,0:T(8,128)(2,1)S(1)}, u32[]{:S(2)}, u32[]{:S(2)}) %collective-permute-start.62) | collective-permute-done | bytes 262176 | tf_op jit(solution)/shard_map/ppermute | solution.py:213
  381.4 12.8 %collective-permute-done.68 = bf16[256,1024]{1,0:T(8,128)(2,1)S(1)} collective-permute-done((bf16[256,1024]{1,0:T(8,128)(2,1)S(1)}, bf16[256,1024]{1,0:T(8,128)(2,1)S(1)}, u32[]{:S(2)}, u32[]{:S(2)}) %collective-permute-start.68) | collective-permute-done | bytes 524320 | tf_op jit(solution)/shard_map/ppermute | solution.py:213
  397.0 8.7 %collective-permute-done.39 = bf16[192,512]{1,0:T(8,128)(2,1)S(1)} collective-permute-done((bf16[192,512]{1,0:T(8,128)(2,1)S(1)}, bf16[192,512]{1,0:T(8,128)(2,1)S(1)}, u32[]{:S(2)}, u32[]{:S(2)}) %collective-permute-start.39) | collective-permute-done | bytes 196640 | tf_op jit(solution)/shard_map/ppermute | solution.py:213
  408.5 23.1 %collective-permute-done.49 = bf16[32,1024]{1,0:T(8,128)(2,1)S(1)} collective-permute-done((bf16[32,1024]{1,0:T(8,128)(2,1)S(1)}, bf16[32,1024]{1,0:T(8,128)(2,1)S(1)}, u32[]{:S(2)}, u32[]{:S(2)}) %collective-permute-start.49) | collective-permute-done | bytes 65568 | tf_op jit(solution)/shard_map/ppermute | solution.py:213
  441.4 13.5 %collective-permute-done.41 = bf16[768,512]{1,0:T(8,128)(2,1)S(1)} collective-permute-done((bf16[768,512]{1,0:T(8,128)(2,1)S(1)}, bf16[768,512]{1,0:T(8,128)(2,1)S(1)}, u32[]{:S(2)}, u32[]{:S(2)}) %collective-permute-start.41) | collective-permute-done | bytes 786464 | tf_op jit(solution)/shard_map/ppermute | solution.py:213
  462.8 6.0 %collective-permute-done.52 = bf16[128,1024]{1,0:T(8,128)(2,1)} collective-permute-done((bf16[128,1024]{1,0:T(8,128)(2,1)}, bf16[128,1024]{1,0:T(8,128)(2,1)}, u32[]{:S(2)}, u32[]{:S(2)}) %collective-permute-start.52) | collective-permute-done | bytes 262176 | tf_op jit(solution)/shard_map/ppermute | solution.py:213
  487.5 6.9 %spread_rows.13 = f32[2048,1024]{1,0:T(8,128)} custom-call(s32[8]{0:T(128)S(1)} %pad_add_fusion.3.order_ref, bf16[1024,1024]{1,0:T(8,128)(2,1)} %pad_maximum_fusion.1.near_ref, bf16[1024,1024]{1,0:T(8,128)(2,1)} %collective-permute-done.70.far_ref), custom_call_target="tpu_custom_call" | custom-call | bytes 12582912 | tf_op jit(solution)/shard_map/spread_rows/pallas_call | solution.py:264
  494.4 5.8 %spread_rows.10 = f32[3072,512]{1,0:T(8,128)} custom-call(s32[8]{0:T(128)S(1)} %pad_add_fusion.3.order_ref, bf16[1536,512]{1,0:T(8,128)(2,1)} %pad_maximum_fusion.2.near_ref, bf16[1536,512]{1,0:T(8,128)(2,1)} %collective-permute-done.42.far_ref), custom_call_target="tpu_custom_call" | custom-call | bytes 9437184 | tf_op jit(solution)/shard_map/spread_rows/pallas_call | solution.py:264
  500.3 6.9 %spread_rows.12 = f32[1024,2048]{1,0:T(8,128)} custom-call(s32[8]{0:T(128)S(1)} %pad_add_fusion.4.order_ref, bf16[512,2048]{1,0:T(8,128)(2,1)} %pad_maximum_fusion.near_ref, bf16[512,2048]{1,0:T(8,128)(2,1)} %collective-permute-done.65.far_ref), custom_call_target="tpu_custom_call" | custom-call | bytes 12582912 | tf_op jit(solution)/shard_map/spread_rows/pallas_call | solution.py:264
  (431 shorter events, 271.9 us)
Async XLA Ops:
  0.7 26.5 %collective-permute-start = (bf16[512,1024]{1,0:T(8,128)(2,1)}, bf16[512,1024]{1,0:T(8,128)(2,1)}, u32[]{:S(2)}, u32[]{:S(2)}) collective-permute-start(bf16[512,1024]{1,0:T(8,128)(2,1)} %param.12), channel_id=1, source_target_pairs={{1,0},{0,1},{3,2},{2,3},{5,4},{4,5},{7,6},{6,7},{9,8},{8,9},{11,10... | collective-permute-start | bytes 3145736 | tf_op jit(solution)/shard_map/ppermute | solution.py:218
  34.7 28.4 %collective-permute-start.4 = (bf16[256,1024]{1,0:T(8,128)(2,1)S(1)}, bf16[256,1024]{1,0:T(8,128)(2,1)S(1)}, u32[]{:S(2)}, u32[]{:S(2)}) collective-permute-start(bf16[256,1024]{1,0:T(8,128)(2,1)S(1)} %constant_dynamic-slice_fusion.15), channel_id=1, source_target_pairs={{1,0},{0,1},{3,2},{2,3},{5,4},{4,5},{7,6},{6,7},{9,8},{8,9},{11,10... | collective-permute-start | bytes 1572872 | tf_op jit(solution)/shard_map/ppermute | solution.py:218
  188.0 24.8 %collective-permute-start.20 = (bf16[512,2048]{1,0:T(8,128)(2,1)}, bf16[512,2048]{1,0:T(8,128)(2,1)}, u32[]{:S(2)}, u32[]{:S(2)}) collective-permute-start(bf16[512,2048]{1,0:T(8,128)(2,1)} %constant_dynamic-slice_fusion.12), channel_id=1, source_target_pairs={{0,2},{2,0},{4,6},{6,4},{8,10},{10,8},{12,14},{14,12},{16,18},{18,... | collective-permute-start | bytes 6291464 | tf_op jit(solution)/shard_map/ppermute | solution.py:213
  188.0 24.8 %collective-permute-start.21 = (bf16[512,2048]{1,0:T(8,128)(2,1)}, bf16[512,2048]{1,0:T(8,128)(2,1)}, u32[]{:S(2)}, u32[]{:S(2)}) collective-permute-start(bf16[512,2048]{1,0:T(8,128)(2,1)} %constant_dynamic-slice_fusion.11), channel_id=1, source_target_pairs={{0,2},{2,0},{4,6},{6,4},{8,10},{10,8},{12,14},{14,12},{16,18},{18,... | collective-permute-start | bytes 6291464 | tf_op jit(solution)/shard_map/ppermute | solution.py:213
  214.6 26.2 %collective-permute-start.23 = (bf16[512,1024]{1,0:T(8,128)(2,1)S(1)}, bf16[512,1024]{1,0:T(8,128)(2,1)}, u32[]{:S(2)}, u32[]{:S(2)}) collective-permute-start(bf16[512,1024]{1,0:T(8,128)(2,1)S(1)} %copy-done.44), channel_id=1, source_target_pairs={{0,4},{2,6},{4,0},{6,2},{8,12},{10,14},{12,8},{14,10},{16,20},{18,... | collective-permute-start | bytes 3145736 | tf_op jit(solution)/shard_map/ppermute | solution.py:213
  215.8 45.0 %collective-permute-start.24 = (bf16[512,1024]{1,0:T(8,128)(2,1)S(1)}, bf16[512,1024]{1,0:T(8,128)(2,1)S(1)}, u32[]{:S(2)}, u32[]{:S(2)}) collective-permute-start(bf16[512,1024]{1,0:T(8,128)(2,1)S(1)} %copy-done.43), channel_id=1, source_target_pairs={{0,4},{2,6},{4,0},{6,2},{8,12},{10,14},{12,8},{14,10},{16,20},{18,... | collective-permute-start | bytes 3145736 | tf_op jit(solution)/shard_map/ppermute | solution.py:213
  220.3 61.9 %collective-permute-start.28 = (bf16[256,2048]{1,0:T(8,128)(2,1)}, bf16[256,2048]{1,0:T(8,128)(2,1)}, u32[]{:S(2)}, u32[]{:S(2)}) collective-permute-start(bf16[256,2048]{1,0:T(8,128)(2,1)} %add_convert_fusion.13), channel_id=1, source_target_pairs={{0,8},{2,10},{4,12},{6,14},{8,0},{10,2},{12,4},{14,6},{16,24},{18,... | collective-permute-start | bytes 3145736 | tf_op jit(solution)/shard_map/ppermute | solution.py:213
  225.6 35.2 %collective-permute-start.25 = (bf16[256,1024]{1,0:T(8,128)(2,1)}, bf16[256,1024]{1,0:T(8,128)(2,1)}, u32[]{:S(2)}, u32[]{:S(2)}) collective-permute-start(bf16[256,1024]{1,0:T(8,128)(2,1)} %constant_dynamic-slice_fusion.10), channel_id=1, source_target_pairs={{0,2},{2,0},{4,6},{6,4},{8,10},{10,8},{12,14},{14,12},{16,18},{18,... | collective-permute-start | bytes 1572872 | tf_op jit(solution)/shard_map/ppermute | solution.py:213
  225.6 35.2 %collective-permute-start.26 = (bf16[256,1024]{1,0:T(8,128)(2,1)}, bf16[256,1024]{1,0:T(8,128)(2,1)}, u32[]{:S(2)}, u32[]{:S(2)}) collective-permute-start(bf16[256,1024]{1,0:T(8,128)(2,1)} %constant_dynamic-slice_fusion.9), channel_id=1, source_target_pairs={{0,2},{2,0},{4,6},{6,4},{8,10},{10,8},{12,14},{14,12},{16,18},{18,... | collective-permute-start | bytes 1572872 | tf_op jit(solution)/shard_map/ppermute | solution.py:213
  240.8 44.1 %collective-permute-start.29 = (bf16[256,2048]{1,0:T(8,128)(2,1)}, bf16[256,2048]{1,0:T(8,128)(2,1)S(1)}, u32[]{:S(2)}, u32[]{:S(2)}) collective-permute-start(bf16[256,2048]{1,0:T(8,128)(2,1)} %add_convert_fusion.12), channel_id=1, source_target_pairs={{0,8},{2,10},{4,12},{6,14},{8,0},{10,2},{12,4},{14,6},{16,24},{18,... | collective-permute-start | bytes 3145736 | tf_op jit(solution)/shard_map/ppermute | solution.py:213
  282.2 174.1 %collective-permute-start.59 = (f32[8192]{0:T(1024)}, f32[8192]{0:T(1024)}, u32[]{:S(2)}, u32[]{:S(2)}) collective-permute-start(f32[8192]{0:T(1024)} %add.571), channel_id=1, source_target_pairs={{0,16},{2,18},{4,20},{6,22},{8,24},{10,26},{12,28},{14,30},{16,0},... | collective-permute-start | bytes 98312 | tf_op jit(solution)/shard_map/ppermute | solution.py:348
  289.1 31.5 %collective-permute-start.32 = (bf16[256,2048]{1,0:T(8,128)(2,1)}, bf16[256,2048]{1,0:T(8,128)(2,1)}, u32[]{:S(2)}, u32[]{:S(2)}) collective-permute-start(bf16[256,2048]{1,0:T(8,128)(2,1)} %add_convert_fusion.10), channel_id=1, source_target_pairs={{0,1},{1,0},{2,3},{3,2},{4,5},{5,4},{6,7},{7,6},{8,9},{9,8},{10,11... | collective-permute-start | bytes 3145736 | tf_op jit(solution)/shard_map/ppermute | solution.py:225
  313.0 51.8 %collective-permute-start.47 = (bf16[128,1024]{1,0:T(8,128)(2,1)S(1)}, bf16[128,1024]{1,0:T(8,128)(2,1)S(1)}, u32[]{:S(2)}, u32[]{:S(2)}) collective-permute-start(bf16[128,1024]{1,0:T(8,128)(2,1)S(1)} %add_convert_fusion.28), channel_id=1, source_target_pairs={{0,1},{1,0},{2,3},{3,2},{4,5},{5,4},{6,7},{7,6},{8,9},{9,8},{10,11... | collective-permute-start | bytes 786440 | tf_op jit(solution)/shard_map/ppermute | solution.py:225
  328.5 25.5 %collective-permute-start.36 = (bf16[768,512]{1,0:T(8,128)(2,1)S(1)}, bf16[768,512]{1,0:T(8,128)(2,1)S(1)}, u32[]{:S(2)}, u32[]{:S(2)}) collective-permute-start(bf16[768,512]{1,0:T(8,128)(2,1)S(1)} %add_convert_fusion.20), channel_id=1, source_target_pairs={{0,4},{2,6},{4,0},{6,2},{8,12},{10,14},{12,8},{14,10},{16,20},{18,... | collective-permute-start | bytes 2359304 | tf_op jit(solution)/shard_map/ppermute | solution.py:213
  339.7 26.6 %collective-permute-start.67 = (bf16[128,1024]{1,0:T(8,128)(2,1)S(1)}, bf16[128,1024]{1,0:T(8,128)(2,1)S(1)}, u32[]{:S(2)}, u32[]{:S(2)}) collective-permute-start(bf16[128,1024]{1,0:T(8,128)(2,1)S(1)} %add_convert_fusion.25), channel_id=1, source_target_pairs={{0,16},{2,18},{4,20},{6,22},{8,24},{10,26},{12,28},{14,30},{16,0},... | collective-permute-start | bytes 786440 | tf_op jit(solution)/shard_map/ppermute | solution.py:213
  339.9 24.8 %collective-permute-start.61 = (bf16[64,2048]{1,0:T(8,128)(2,1)S(1)}, bf16[64,2048]{1,0:T(8,128)(2,1)S(1)}, u32[]{:S(2)}, u32[]{:S(2)}) collective-permute-start(bf16[64,2048]{1,0:T(8,128)(2,1)S(1)} %constant_dynamic-slice_fusion), channel_id=1, source_target_pairs={{0,16},{2,18},{4,20},{6,22},{8,24},{10,26},{12,28},{14,30},{16,0},... | collective-permute-start | bytes 786440 | tf_op jit(solution)/shard_map/ppermute | solution.py:213
  366.3 28.0 %collective-permute-start.68 = (bf16[256,1024]{1,0:T(8,128)(2,1)S(1)}, bf16[256,1024]{1,0:T(8,128)(2,1)S(1)}, u32[]{:S(2)}, u32[]{:S(2)}) collective-permute-start(bf16[256,1024]{1,0:T(8,128)(2,1)S(1)} %pad_maximum_fusion.8), channel_id=1, source_target_pairs={{0,8},{2,10},{4,12},{6,14},{8,0},{10,2},{12,4},{14,6},{16,24},{18,... | collective-permute-start | bytes 1572872 | tf_op jit(solution)/shard_map/ppermute | solution.py:213
  394.3 40.9 %collective-permute-start.69 = (bf16[512,1024]{1,0:T(8,128)(2,1)S(1)}, bf16[512,1024]{1,0:T(8,128)(2,1)S(1)}, u32[]{:S(2)}, u32[]{:S(2)}) collective-permute-start(bf16[512,1024]{1,0:T(8,128)(2,1)S(1)} %pad_maximum_fusion.4), channel_id=1, source_target_pairs={{0,4},{2,6},{4,0},{6,2},{8,12},{10,14},{12,8},{14,10},{16,20},{18,... | collective-permute-start | bytes 3145736 | tf_op jit(solution)/shard_map/ppermute | solution.py:213
  395.1 43.1 %collective-permute-start.64 = (bf16[256,2048]{1,0:T(8,128)(2,1)S(1)}, bf16[256,2048]{1,0:T(8,128)(2,1)S(1)}, u32[]{:S(2)}, u32[]{:S(2)}) collective-permute-start(bf16[256,2048]{1,0:T(8,128)(2,1)S(1)} %pad_maximum_fusion.3), channel_id=1, source_target_pairs={{0,8},{2,10},{4,12},{6,14},{8,0},{10,2},{12,4},{14,6},{16,24},{18,... | collective-permute-start | bytes 3145736 | tf_op jit(solution)/shard_map/ppermute | solution.py:213
  405.7 28.3 %collective-permute-start.40 = (bf16[384,512]{1,0:T(8,128)(2,1)S(1)}, bf16[384,512]{1,0:T(8,128)(2,1)S(1)}, u32[]{:S(2)}, u32[]{:S(2)}) collective-permute-start(bf16[384,512]{1,0:T(8,128)(2,1)S(1)} %pad_maximum_fusion.9), channel_id=1, source_target_pairs={{0,8},{2,10},{4,12},{6,14},{8,0},{10,2},{12,4},{14,6},{16,24},{18,... | collective-permute-start | bytes 1179656 | tf_op jit(solution)/shard_map/ppermute | solution.py:213
  405.8 25.8 %collective-permute-start.49 = (bf16[32,1024]{1,0:T(8,128)(2,1)S(1)}, bf16[32,1024]{1,0:T(8,128)(2,1)S(1)}, u32[]{:S(2)}, u32[]{:S(2)}) collective-permute-start(bf16[32,1024]{1,0:T(8,128)(2,1)S(1)} %constant_dynamic-slice_fusion.2), channel_id=1, source_target_pairs={{0,16},{2,18},{4,20},{6,22},{8,24},{10,26},{12,28},{14,30},{16,0},... | collective-permute-start | bytes 196616 | tf_op jit(solution)/shard_map/ppermute | solution.py:213
  438.2 49.3 %collective-permute-start.70 = (bf16[1024,1024]{1,0:T(8,128)(2,1)}, bf16[1024,1024]{1,0:T(8,128)(2,1)}, u32[]{:S(2)}, u32[]{:S(2)}) collective-permute-start(bf16[1024,1024]{1,0:T(8,128)(2,1)} %pad_maximum_fusion.1.near_ref), channel_id=1, source_target_pairs={{0,2},{2,0},{4,6},{6,4},{8,10},{10,8},{12,14},{14,12},{16,18},{18,... | collective-permute-start | bytes 6291464 | tf_op jit(solution)/shard_map/ppermute | solution.py:213
  439.7 60.6 %collective-permute-start.65 = (bf16[512,2048]{1,0:T(8,128)(2,1)}, bf16[512,2048]{1,0:T(8,128)(2,1)}, u32[]{:S(2)}, u32[]{:S(2)}) collective-permute-start(bf16[512,2048]{1,0:T(8,128)(2,1)} %pad_maximum_fusion.near_ref), channel_id=1, source_target_pairs={{0,2},{2,0},{4,6},{6,4},{8,10},{10,8},{12,14},{14,12},{16,18},{18,... | collective-permute-start | bytes 6291464 | tf_op jit(solution)/shard_map/ppermute | solution.py:213
  456.3 38.2 %collective-permute-start.42 = (bf16[1536,512]{1,0:T(8,128)(2,1)}, bf16[1536,512]{1,0:T(8,128)(2,1)}, u32[]{:S(2)}, u32[]{:S(2)}) collective-permute-start(bf16[1536,512]{1,0:T(8,128)(2,1)} %pad_maximum_fusion.2.near_ref), channel_id=1, source_target_pairs={{0,2},{2,0},{4,6},{6,4},{8,10},{10,8},{12,14},{14,12},{16,18},{18,... | collective-permute-start | bytes 4718600 | tf_op jit(solution)/shard_map/ppermute | solution.py:213
  (120 other events, 1128.7 us)

commit v2 on v1

--- a/solution.py
+++ b/solution.py
@@ -76,9 +76,11 @@
     lse_ref,
     seen_ref,
     bar_ref,
-    *refs,
+    grad_own_ref,
+    grad_rest_ref,
+    key_acc,
+    value_acc,
 ):
-    grad_own_ref, grad_rest_ref, key_acc, value_acc = refs[-4:]
     lane = lax.broadcasted_iota(jnp.int32, (1, 128), 1)
     rows_own = own_ref.shape[1]
     rows = rows_own + rest_ref.shape[1]
@@ -153,18 +155,14 @@
         input_output_aliases={4: 0, 5: 1} if previous else {},
         compiler_params=pltpu.CompilerParams(vmem_limit_bytes=VMEM_ASK),
         cost_estimate=pl.CostEstimate(
-            flops=count * 16 * 256 * rows * rows,
-            transcendentals=count * 2 * rows * rows,
-            bytes_accessed=count * 10 * 128 * rows,
+            flops=count * rows * rows, transcendentals=0, bytes_accessed=count * rows
         ),
         name="attn_forward",
     )(own, rest, seen, bar, *previous)
 
 
-def attn_backward(
-    own, rest, up_own, up_rest, mixed, lse, seen, bar, scale, block, start, count, previous=()
-):
-    rows_own, rows_rest, width = own.shape[1], rest.shape[1], own.shape[2]
+def attn_backward(own, rest, up_own, up_rest, mixed, lse, seen, bar, scale, block, start, count):
+    rows_own, rows_rest = own.shape[1], rest.shape[1]
     rows = rows_own + rows_rest
     return pl.pallas_call(
         functools.partial(attn_backward_kernel, block, scale),
@@ -178,26 +176,22 @@
             pl.BlockSpec((1, 8, rows), lambda p: (p + start, 0, 0)),
             pl.BlockSpec((rows, 128), lambda p: (0, 0)),
             pl.BlockSpec((rows, 128), lambda p: (0, 0)),
-        ]
-        + [pl.BlockSpec(memory_space=pl.ANY)] * len(previous),
+        ],
         out_specs=[
-            pl.BlockSpec((3, rows_own, 128), lambda p: (0, 0, p + start)),
-            pl.BlockSpec((3, rows_rest, 128), lambda p: (0, 0, p + start)),
+            pl.BlockSpec((3, rows_own, 128), lambda p: (0, 0, p)),
+            pl.BlockSpec((3, rows_rest, 128), lambda p: (0, 0, p)),
         ],
         out_shape=[
-            jax.ShapeDtypeStruct((3, rows_own, width), jnp.bfloat16),
-            jax.ShapeDtypeStruct((3, rows_rest, width), jnp.bfloat16),
+            jax.ShapeDtypeStruct((3, rows_own, count * 128), jnp.bfloat16),
+            jax.ShapeDtypeStruct((3, rows_rest, count * 128), jnp.bfloat16),
         ],
-        input_output_aliases={8: 0, 9: 1} if previous else {},
         scratch_shapes=[pltpu.VMEM((rows, 128), jnp.float32)] * 2,
         compiler_params=pltpu.CompilerParams(vmem_limit_bytes=VMEM_ASK),
         cost_estimate=pl.CostEstimate(
-            flops=count * 24 * 256 * rows * rows,
-            transcendentals=count * 2 * rows * rows,
-            bytes_accessed=count * 18 * 128 * rows,
+            flops=count * rows * rows, transcendentals=0, bytes_accessed=count * rows
         ),
         name="attn_backward",
-    )(own, rest, up_own, up_rest, mixed, lse, seen, bar, *previous)
+    )(own, rest, up_own, up_rest, mixed, lse, seen, bar)
 
 
 def doc_features(docs):
@@ -232,14 +226,15 @@
     return lax.optimization_barrier(trees)
 
 
-def spread_kernel(count, order_ref, near_ref, far_ref, out_ref):
+def spread_kernel(count, order_ref, near_ref, far_ref, *refs):
+    out_ref = refs[-1]
     step = pl.program_id(0)
-    rows = near_ref.shape[0] // count
+    rows = near_ref.shape[1] // count
 
     def store(ref):
         for index in range(count):
             offset = pl.multiple_of(order_ref[4 + index] * rows, rows)
-            out_ref[pl.ds(offset, rows)] = ref[index * rows : (index + 1) * rows].astype(
+            out_ref[:, pl.ds(offset, rows)] = ref[:, index * rows : (index + 1) * rows].astype(
                 out_ref.dtype
             )
 
@@ -252,8 +247,8 @@
         store(far_ref)
 
 
-def spread(near, far, place, count, kind):
-    rows, columns = near.shape[0] // 2, near.shape[1]
+def spread(near, far, place, count, kind, column=0, columns_all=None, previous=()):
+    lead, rows, columns = near.shape[0], near.shape[1] // 2, near.shape[2]
     quarter, inner = lax.div(place, jnp.int32(count)), lax.rem(place, jnp.int32(count))
     order = jnp.concatenate(
         [
@@ -261,24 +256,27 @@
             jnp.bitwise_xor(inner, jnp.arange(count, dtype=jnp.int32)),
         ]
     )
+    block = (lead, rows, columns)
     return pl.pallas_call(
         functools.partial(spread_kernel, count),
         grid_spec=pltpu.PrefetchScalarGridSpec(
             num_scalar_prefetch=1,
             grid=(4,),
             in_specs=[
-                pl.BlockSpec((rows, columns), lambda step, order: (jnp.minimum(step, 1), 0)),
-                pl.BlockSpec((rows, columns), lambda step, order: (jnp.maximum(step - 2, 0), 0)),
-            ],
-            out_specs=pl.BlockSpec((rows, columns), lambda step, order: (order[step], 0)),
+                pl.BlockSpec(block, lambda step, order: (0, jnp.minimum(step, 1), 0)),
+                pl.BlockSpec(block, lambda step, order: (0, jnp.maximum(step - 2, 0), 0)),
+            ]
+            + [pl.BlockSpec(memory_space=pl.ANY)] * len(previous),
+            out_specs=pl.BlockSpec(block, lambda step, order: (0, order[step], column)),
         ),
-        out_shape=jax.ShapeDtypeStruct((4 * rows, columns), kind),
+        out_shape=jax.ShapeDtypeStruct((lead, 4 * rows, columns_all or columns), kind),
+        input_output_aliases={3: 0} if previous else {},
         compiler_params=pltpu.CompilerParams(vmem_limit_bytes=VMEM_ASK // 2),
         cost_estimate=pl.CostEstimate(
-            flops=0, transcendentals=0, bytes_accessed=24 * rows * columns
+            flops=0, transcendentals=0, bytes_accessed=24 * lead * rows * columns
         ),
         name="spread_rows",
-    )(order, near, far)
+    )(order, near, far, *previous)
 
 
 def bit_of(dp_pos, mask):
@@ -286,8 +284,8 @@
 
 
 def half_of(array, index):
-    rows = array.shape[0] // 2
-    return lax.dynamic_slice_in_dim(array, index * rows, rows, 0)
+    rows = array.shape[1] // 2
+    return lax.dynamic_slice_in_dim(array, index * rows, rows, 1)
 
 
 def opening(parts, dp_pos, mask):
@@ -332,13 +330,14 @@
     return array
 
 
-def gather_rows(mine, dp_pos, masks):
+def gather_rows(mine, dp_pos, masks, *where):
     for mask in reversed(masks[1:]):
-        mine = jnp.concatenate([mine, xor_step(mine, mask)], axis=0)
+        mine = jnp.concatenate([mine, xor_step(mine, mask)], axis=1)
     place = jnp.int32(0)
     for mask in masks:
         place = 2 * place + bit_of(dp_pos, mask)
-    return spread(mine, xor_step(mine, masks[0]), place, 2 ** (len(masks) - 2), jnp.float32)
+    far = xor_step(mine, masks[0])
+    return spread(mine, far, place, 2 ** (len(masks) - 2), jnp.float32, *where)
 
 
 def butterfly(array, axis):
@@ -377,6 +376,7 @@
     masks = [2**k for k in range(count_dp.bit_length() - 1)]
     masks_up = [masks[0], masks[2], masks[1]] + masks[3:]
     others = range(1, ranks)
+    same_core = [[i for i in range(count_dp) if i % 2 == side] for side in range(2)]
 
     rest = [from_rank(tokens, ahead) for ahead in others]
     rest = rest[0] if ranks == 2 else jnp.concatenate(rest, axis=0)
@@ -401,11 +401,7 @@
         )
 
     out_place = 2 * bit_of(dp_pos, 1) + bit_of(dp_pos, 2)
-    out_first, up_first, down_first = (
-        slice_from(out_own, 4, out_place),
-        slice_from(up_own, 8, place),
-        slice_from(down_own, 8, place),
-    )
+    out_first, up_first = slice_from(out_own, 4, out_place), slice_from(up_own, 8, place)
     docs = [
         lax.dynamic_slice_in_dim(
             doc_ids, lax.rem(tensor_pos + ahead, ranks) * rows_own, rows_own, 0
@@ -420,29 +416,33 @@
         return (wide + bias).astype(low)
 
     qkv_own, qkv_rest = project(tokens), project(rest)
+    qkv_rest, down_own, out_first = meet(qkv_rest, down_own, out_first)
+    down_first = slice_from(down_own, 8, place)
+    out_second = send(out_first, 2)
     pairs = width // 128
     early = max(1, pairs // 2)
     block = min(512, rows_own)
     mixed_lse = attn_forward(qkv_own, qkv_rest, seen, bar, scale, block, 0, early)
-    mixed_lse, out_first, up_first = meet(mixed_lse, out_first, up_first)
-    out_second = send(out_first, 2)
+    mixed_lse, out_second, up_first = meet(mixed_lse, out_second, up_first)
     up_second, up_third = send(up_first, 2), send(up_first, 4)
     if pairs > early:
         mixed_lse = attn_forward(
             qkv_own, qkv_rest, seen, bar, scale, block, early, pairs - early, tuple(mixed_lse)
         )
-    mixed_lse, out_second, down_first = meet(mixed_lse, out_second, down_first)
     out_half = joined([out_first, out_second])
     out_far = send(out_half, 1)
+    mixed_lse, down_first = meet(mixed_lse, down_first)
     down_second, down_third = send(down_first, 2), send(down_first, 4)
     mixed, lse = mixed_lse
     mixed_parts = [mixed[k * rows_own : (k + 1) * rows_own] for k in range(ranks)]
     mixed_got = exchange(mixed_parts)
     mixed_got[0] = mixed_parts[0]
-    mixed_got, out_far, up_second, up_third = meet(mixed_got, out_far, up_second, up_third)
+    mixed_got, out_far, up_second, up_third, up_biases = meet(
+        mixed_got, out_far, up_second, up_third, up_biases
+    )
     up_corner = corner(up_second, up_third)
     outs = [out_own] + [
-        spread(near, far, out_place, 1, low) for near, far in zip(out_half, out_far, strict=True)
+        spread(near[None], far[None], out_place, 1, low)[0] for near, far in zip(out_half, out_far, strict=True)
     ]
     attention = sum(
         jnp.dot(mixed_got[k], outs[k], preferred_element_type=jnp.float32) for k in range(ranks)
@@ -459,28 +459,29 @@
         density = jnp.exp(-0.5 * hidden * hidden) * GAUSS_NORM
         return meet((hidden * below).astype(low), (below + hidden * density).astype(low))
 
-    normed_low, up_corner, down_second, down_third = meet(
-        normed_low, up_corner, down_second, down_third
+    pairs_active = [activate(up_own, up_bias)]
+    pairs_active, up_corner, down_second, down_third = meet(
+        pairs_active, up_corner, down_second, down_third
     )
     up_half = joined([up_first, up_second, up_third, *up_corner])
     up_far = send(up_half, 1)
     down_corner = corner(down_second, down_third)
-    pairs_active = [activate(up_own, up_bias)]
-    pairs_active, up_far = meet(pairs_active, up_far)
-    ups = [up_own] + [
-        spread(near, far, place, 2, low) for near, far in zip(up_half, up_far, strict=True)
-    ]
-    ups, down_corner = meet(ups, down_corner)
+    branch = jnp.dot(pairs_active[0][0], down_own, preferred_element_type=jnp.float32)
+    branch, up_far, down_corner = meet(branch, up_far, down_corner)
     down_half = joined([down_first, down_second, down_third, *down_corner])
     down_far = send(down_half, 1)
+    ups = [up_own] + [
+        spread(near[None], far[None], place, 2, low)[0]
+        for near, far in zip(up_half, up_far, strict=True)
+    ]
     pairs_active += [activate(ups[k], up_biases[k]) for k in others]
     pairs_active, down_far = meet(pairs_active, down_far)
     downs = [down_own] + [
-        spread(near, far, place, 2, low) for near, far in zip(down_half, down_far, strict=True)
+        spread(near[None], far[None], place, 2, low)[0]
+        for near, far in zip(down_half, down_far, strict=True)
     ]
     active, slope = zip(*pairs_active, strict=True)
-    branch = 0.0
-    for k in range(ranks):
+    for k in others:
         branch = branch + jnp.dot(active[k], downs[k], preferred_element_type=jnp.float32)
     result, unit_second, inverse_second = norm_forward(
         normed + branch + out_biases[1], ln_gains[1], ln_shifts[1]
@@ -499,7 +500,7 @@
         for k in range(ranks)
     ]
     down_parts, branch_grad = meet(down_parts, branch_grad)
-    down_away, down_keep = opening(down_parts, dp_pos, masks[0])
+    down_away, down_keep = opening([part[None] for part in down_parts], dp_pos, masks[0])
     down_away, branch_grad = meet(down_away, branch_grad)
     down_got = send(down_away, masks[0])
     hidden_grads = []
@@ -509,56 +510,50 @@
         )
         hidden_grads.append((active_grad * slope[k].astype(jnp.float32)).astype(low))
     hidden_grads, down_got = meet(hidden_grads, down_got)
-    down_away, down_keep = fold(down_keep, down_got, dp_pos, masks[1])
-    down_away, hidden_grads = meet(down_away, hidden_grads)
-    down_got = send(down_away, masks[1])
+    down_sums = add(down_keep, down_got)
+    down_sums, hidden_grads = meet(down_sums, hidden_grads)
+    down_got = exchange(down_sums)[1:]
+    normed_grad = second_grad
+    for k in range(ranks):
+        normed_grad = normed_grad + jnp.einsum(
+            "sf,df->sd", hidden_grads[k], ups[k], preferred_element_type=jnp.float32
+        )
+    first_grad, gain_grad_first, shift_grad_first = norm_backward(
+        normed_grad, unit_first, inverse_first, ln_gains[0]
+    )
+    bias_grad_first = jnp.sum(first_grad, axis=0)
+    attn_grad = first_grad.astype(low)
+    mixed_grads = [
+        jnp.einsum("sd,cd->sc", attn_grad, outs[k], preferred_element_type=jnp.float32).astype(low)
+        for k in range(ranks)
+    ]
+    grads_got = exchange(mixed_grads)[1:]
     up_parts = [
         jnp.einsum(
             "sd,sf->df", normed_low, hidden_grads[k], preferred_element_type=jnp.float32
         ).astype(low)
         for k in range(ranks)
     ]
-    up_away, up_keep = opening(up_parts, dp_pos, masks_up[0])
-    up_away, hidden_grads = meet(up_away, hidden_grads)
+    up_away, up_keep = opening([part[None] for part in up_parts], dp_pos, masks_up[0])
     up_got = send(up_away, masks_up[0])
-    normed_grad = second_grad
-    for k in range(ranks):
-        normed_grad = normed_grad + jnp.einsum(
-            "sf,df->sd", hidden_grads[k], ups[k], preferred_element_type=jnp.float32
-        )
-    first_grad, gain_grad_first, shift_grad_first = norm_backward(
-        normed_grad, unit_first, inverse_first, ln_gains[0]
-    )
-    bias_grad_first = jnp.sum(first_grad, axis=0)
-    attn_grad = first_grad.astype(low)
-    mixed_grads = [
-        jnp.einsum("sd,cd->sc", attn_grad, outs[k], preferred_element_type=jnp.float32).astype(low)
-        for k in range(ranks)
-    ]
-    mixed_grads, up_got = meet(mixed_grads, up_got)
-    grads_got = exchange(mixed_grads)
-    up_away, up_keep = fold(up_keep, up_got, dp_pos, masks_up[1])
-    up_got = send(up_away, masks_up[1])
     out_parts = [
         jnp.einsum("sc,sd->cd", mixed_got[k], attn_grad, preferred_element_type=jnp.float32).astype(
             low
         )
         for k in range(ranks)
     ]
-    out_away, out_keep = opening(out_parts, dp_pos, masks[0])
-    out_away, grads_got = meet(out_away, grads_got[1:])
+
+    out_away, out_keep = opening([part[None] for part in out_parts], dp_pos, masks[0])
+    out_away, up_got, grads_got = meet(out_away, up_got, grads_got)
     out_got = send(out_away, masks[0])
+    up_away, up_keep = fold(up_keep, up_got, dp_pos, masks_up[1])
+    up_away, mixed_grads, grads_got = meet(up_away, mixed_grads, grads_got)
+    up_got = send(up_away, masks_up[1])
     grads_rest = grads_got[0] if ranks == 2 else jnp.concatenate(grads_got, axis=0)
     block = min(256, rows_own)
-    qkv_grads = attn_backward(
-        qkv_own, qkv_rest, mixed_grads[0], grads_rest, mixed, lse, seen, bar, scale, block, 0, early
-    )
-    qkv_grads, down_got, out_got = meet(qkv_grads, down_got, out_got)
-    down_keep, down_got = fold_ranks(down_keep, down_got)
-    out_away, out_keep = fold(out_keep, out_got, dp_pos, masks[1])
-    out_got = send(out_away, masks[1])
-    if pairs > early:
-        qkv_grads = attn_backward(
+
+    def backward(start, count):
+        return attn_backward(
             qkv_own,
             qkv_rest,
             mixed_grads[0],
@@ -569,75 +564,114 @@
             bar,
             scale,
             block,
-            early,
-            pairs - early,
-            tuple(qkv_grads),
-        )
-    qkv_grads, down_got, up_got, out_got = meet(qkv_grads, down_got, up_got, out_got)
-    down_sum = add_ranks(down_keep, down_got)
-    down_away, down_keep = opening([down_sum], dp_pos, masks[2])
-    down_got = send(down_away, masks[2])
+            start,
+            count,
+        )
+
+    def open_qkv(chunk):
+        own, far = chunk
+        total = jnp.einsum("sd,isc->idc", rest, far, preferred_element_type=jnp.float32)
+        total = total + jnp.einsum("sd,isc->idc", tokens, own, preferred_element_type=jnp.float32)
+        return opening([total.astype(low)], dp_pos, masks[0])
+
+    chunks = [backward(0, early)]
+    chunks, out_got = meet(chunks, out_got)
+    out_keep, out_got = fold_ranks(out_keep, out_got)
+    qkv_away, qkv_keep = open_qkv(chunks[0])
+    qkv_state = [(qkv_keep, send(qkv_away, masks[0]))]
+    if pairs > early:
+        chunks, qkv_away, grads_rest = meet(chunks, qkv_away, grads_rest)
+        chunks = [chunks[0], backward(early, pairs - early)]
+        chunks, qkv_state = meet(chunks, qkv_state)
+        keep, got = qkv_state[0]
+        qkv_away, qkv_keep = fold(keep, got, dp_pos, masks[1])
+        qkv_state = [(qkv_keep, send(qkv_away, masks[1]))]
+        qkv_away, qkv_keep = open_qkv(chunks[1])
+        qkv_away, down_got, out_got = meet(qkv_away, down_got, out_got)
+        halves = lax.psum(
+            (add_ranks([down_sums[0]], down_got), add_ranks(out_keep, out_got)),
+            "dp",
+            axis_index_groups=same_core,
+        )
+        qkv_state.append((qkv_keep, send(qkv_away, masks_up[0])))
+    else:
+        halves = lax.psum(
+            (add_ranks([down_sums[0]], down_got), add_ranks(out_keep, out_got)),
+            "dp",
+            axis_index_groups=same_core,
+        )
+        keep, got = qkv_state[0]
+        qkv_away, qkv_keep = fold(keep, got, dp_pos, masks[1])
+        qkv_state = [(qkv_keep, send(qkv_away, masks[1]))]
     up_keep, up_got = fold_ranks(up_keep, up_got)
-    out_keep, out_got = fold_ranks(out_keep, out_got)
-    qkv_grad_own, qkv_grad_rest = qkv_grads
-
-    def input_part(item):
-        return jnp.einsum("isc,idc->sd", item, w_qkv, preferred_element_type=jnp.float32)
-
-    grad_qkv = jnp.einsum("sd,isc->idc", rest, qkv_grad_rest, preferred_element_type=jnp.float32)
-    grad_qkv = grad_qkv + jnp.einsum(
-        "sd,isc->idc", tokens, qkv_grad_own, preferred_element_type=jnp.float32
-    )
-    qkv_away, qkv_keep = opening([grad_qkv.astype(low).reshape(3 * D, width)], dp_pos, masks[0])
-    qkv_got = send(qkv_away, masks[0])
-    far = input_part(qkv_grad_rest).astype(low)
-    far, qkv_got, down_got = meet(far, qkv_got, down_got)
-    qkv_away, qkv_keep = fold(qkv_keep, qkv_got, dp_pos, masks[1])
-    qkv_got = send(qkv_away, masks[1])
-    down_sum = scatter_on(add(down_keep, down_got)[0], dp_pos, masks[3:])
-    near = input_part(qkv_grad_own)
+
+    edges = [0, early * 128, width]
+
+    def input_part(side):
+        total = 0.0
+        for index, chunk in enumerate(chunks):
+            total = total + jnp.einsum(
+                "isc,idc->sd",
+                chunk[side],
+                w_qkv[:, :, edges[index] : edges[index + 1]],
+                preferred_element_type=jnp.float32,
+            )
+        return total
+
+    if pairs > early:
+        keep, got = qkv_state[1]
+        qkv_away, qkv_keep = fold(keep, got, dp_pos, masks_up[1])
+        qkv_state[1] = (qkv_keep, send(qkv_away, masks_up[1]))
+    far = input_part(1).astype(low)
+    near = input_part(0)
     near, up_got, far = meet(near, up_got, far)
     inputs_got = exchange(
         [None] + [far[k * rows_own : (k + 1) * rows_own] for k in range(ranks - 1)]
     )
     up_sum = scatter_on(add_ranks(up_keep, up_got), dp_pos, masks_up[2:])
-    qkv_sum = scatter_on(add(qkv_keep, qkv_got)[0], dp_pos, masks[2:])
-    grad_down = gather_rows(down_sum, dp_pos, masks)
-    grad_up = gather_rows(up_sum, dp_pos, masks_up)
-    grad_qkv = gather_rows(qkv_sum, dp_pos, masks)
-    out_sum = add_ranks(out_keep, out_got)
-    if (out_sum.shape[0] * 4 // count_dp) % 16 == 0:
-        grad_out = gather_rows(scatter_on(out_sum, dp_pos, masks[2:]), dp_pos, masks)
-    else:
-        for mask in masks[2:]:
-            out_sum = add([out_sum], send([out_sum], mask))[0]
-        half = jnp.concatenate([out_sum, xor_step(out_sum, masks[1])], axis=0)
-        grad_out = spread(half, xor_step(half, masks[0]), out_place, 1, jnp.float32)
-
-    up_sums = [jnp.sum(item.astype(jnp.float32), axis=0) for item in hidden_grads]
-    sums_got = exchange(up_sums)
-    hidden_sum = up_sums[0]
-    for piece in sums_got[1:]:
+    orders = [masks, masks_up]
+    qkv_sums = [
+        scatter_on(add(*state)[0], dp_pos, order[2:])
+        for state, order in zip(qkv_state, orders[: len(chunks)], strict=True)
+    ]
+    grad_up = gather_rows(up_sum, dp_pos, masks_up)[0]
+    grad_qkv = gather_rows(qkv_sums[0], dp_pos, masks, 0, width)
+    if pairs > early:
+        grad_qkv = gather_rows(qkv_sums[1], dp_pos, masks_up, 1, width, (grad_qkv,))
+    halves, grad_qkv, grad_up = meet(halves, grad_qkv, grad_up)
+    core_place = 2 * bit_of(dp_pos, masks[0])
+    grad_down, grad_out = [
+        spread(half, xor_step(half, masks[0]), core_place, 1, jnp.float32)[0] for half in halves
+    ]
+    column_sums = jnp.concatenate(
+        [
+            jnp.sum(own.astype(jnp.float32), axis=1) + jnp.sum(far.astype(jnp.float32), axis=1)
+            for own, far in chunks
+        ],
+        axis=1,
+    )
+    hidden_sums = [jnp.sum(item.astype(jnp.float32), axis=0) for item in hidden_grads]
+    shared = jnp.concatenate(
+        [
+            bias_grad_first,
+            bias_grad_second,
+            gain_grad_first,
+            gain_grad_second,
+            shift_grad_first,
+            shift_grad_second,
+        ]
+    )
+    shared, hidden_sums, chunks = meet(shared, hidden_sums, chunks)
+    shared = butterfly(shared, "tensor")
+    hidden_sum = hidden_sums[0]
+    for piece in exchange(hidden_sums)[1:]:
         hidden_sum = hidden_sum + piece
-    shared = butterfly(
-        jnp.stack(
-            [
-                bias_grad_first,
-                bias_grad_second,
-                gain_grad_first,
-                gain_grad_second,
-                shift_grad_first,
-                shift_grad_second,
-            ]
-        ),
-        "tensor",
-    )
-    shared = butterfly(jnp.concatenate([shared.reshape(-1), hidden_sum]), "dp")
-    shared, grad_up_bias = shared[: 6 * D].reshape(6, D), shared[6 * D :]
-    qkv_sums = jnp.sum(qkv_grad_own.astype(jnp.float32), axis=1) + jnp.sum(
-        qkv_grad_rest.astype(jnp.float32), axis=1
-    )
-    grad_qv = butterfly(jnp.stack([qkv_sums[0], qkv_sums[2]]), "dp")
+    cuts = [6 * D, 6 * D + hidden_sum.shape[0], 6 * D + hidden_sum.shape[0] + width]
+    sums = butterfly(
+        jnp.concatenate([shared, hidden_sum, column_sums[0], column_sums[2]]), "dp"
+    )
+    shared, grad_up_bias = sums[: cuts[0]].reshape(6, D), sums[cuts[0] : cuts[1]]
+    grad_qv = sums[cuts[1] :].reshape(2, width)
     grad_input = first_grad + near
     for piece in inputs_got[1:]:
         grad_input = grad_input + piece.astype(jnp.float32)

time: 512 us -> 547 us (1.068)
  waiting for transfers between devices: 177 us -> 249 us
  starting transfers between devices: 70.6 us -> 54.4 us
  local copies, waits for them, and re-layouts: 51.9 us -> 37.9 us
  between operations: 2.12 us -> 15.8 us
  other arithmetic: 58.7 us -> 47.8 us
  Pallas kernels: 73.9 us -> 67.1 us
    ppermute x7, waiting for transfers between devices: 9.09 us -> 73.3 us  [exchange(): lax.ppermute(parts[ahead], 'tensor', [(i, (i + ahead) % size) for i in ra...]
    psum x0 -> x1, waiting for transfers between devices: none -> 25.2 us  [shards(): lax.psum((add_ranks([down_sums[0]], down_got), add_ranks(out_keep, out_go...]
    ppermute x50 -> x44, waiting for transfers between devices: 142 us -> 122 us  [xor_step(): return lax.ppermute(array, 'dp', [(i, i ^ mask) for i in range(size)])]
    ppermute x50 -> x44, starting transfers between devices: 45.4 us -> 31 us  [xor_step(): return lax.ppermute(array, 'dp', [(i, i ^ mask) for i in range(size)])]
    ppermute x9 -> x5, waiting for transfers between devices: 3.07 us -> 11.5 us  [butterfly(): lax.ppermute(array, axis, [(i, i ^ mask) for i in range(size)])]
    pallas_call x7 -> x8, Pallas kernels: 32.3 us -> 25.4 us  [spread(): pl.pallas_call(functools.partial(spread_kernel, count), grid_spec=pltpu.P...]
    ppermute x5, waiting for transfers between devices: 23.1 us -> 17.3 us  [from_rank(): lax.ppermute(array, 'tensor', [((i + ahead) % size, i) for i in range(siz...]
    dot_general x4 -> x9, matrix products: 12.5 us -> 16.6 us  [the longest x4 6.38 us: input_part(): jnp.einsum('isc,idc->sd', chunk[side], w_qkv[:, :, edges[index]:edges[ind...]
  transfers between devices with their start and end apart: 71 -> 62, of which waited for: 27 -> 27; matrix products, arithmetic and copies ran while one was open for 25% -> 20% of each run, Pallas kernels for 12% -> 10%
where the time goes in v2:
time: 547 us; the launch traced here: 542 us
  waiting for transfers between devices  249 us (46%)
  matrix products  69.9 us (13%)
  Pallas kernels  67.1 us (12%)
  starting transfers between devices  54.4 us (10%)
  other arithmetic  47.8 us (9%)
  local copies, waits for them, and re-layouts  37.9 us (7%)
  between operations  15.8 us (3%)
    ppermute x44, waiting for transfers between devices, xor_step(): return lax.ppermute(array, 'dp', [(i, i ^ mask) for i in range(size)])  122 us
    ppermute x7, waiting for transfers between devices, exchange(): lax.ppermute(parts[ahead], 'tensor', [(i, (i + ahead) % size) for i in ra...  73.3 us
    ppermute x44, starting transfers between devices, xor_step(): return lax.ppermute(array, 'dp', [(i, i ^ mask) for i in range(size)])  31 us
    pallas_call x8, Pallas kernels, spread(): pl.pallas_call(functools.partial(spread_kernel, count), grid_spec=pltpu.P...  25.4 us
    psum x1, waiting for transfers between devices, shards(): lax.psum((add_ranks([down_sums[0]], down_got), add_ranks(out_keep, out_go...  25.2 us
    pallas_call x2, Pallas kernels, attn_backward(): pl.pallas_call(functools.partial(attn_backward_kernel, block, scale), gri...  24.4 us
    unnamed x176, local copies, waits for them, and re-layouts  22.3 us
    convert_element_type x16, other arithmetic, add(): (a.astype(jnp.float32) + b.astype(jnp.float32)).astype(a.dtype)  19.8 us
  transfers between devices with their start and end apart: 62, of which 27 were waited for; matrix products, arithmetic and copies ran while one was open for 20% of the time, Pallas kernels for 10%

profile of v2, /device:TPU:0, one launch (start us, length us, event | category | flops | bytes accessed | tf_op | source)
XLA Modules:
  0.0 542.2 jit_solution(12985304631601811659)
XLA Ops:
  19.3 14.5 %collective-permute-done = bf16[512,1024]{1,0:T(8,128)(2,1)} collective-permute-done((bf16[512,1024]{1,0:T(8,128)(2,1)}, bf16[512,1024]{1,0:T(8,128)(2,1)}, u32[]{:S(2)}, u32[]{:S(2)}) %collective-permute-start) | collective-permute-done | bytes 1048608 | tf_op jit(solution)/shard_map/ppermute | solution.py:212
  46.5 8.9 %attn_forward.2 = (bf16[1024,512]{1,0:T(8,128)(2,1)S(1)}, f32[4,8,1024]{2,1,0:T(8,128)S(1)}) custom-call(bf16[3,512,512]{2,1,0:T(8,128)(2,1)S(1)} %fusion.29.own_ref, bf16[3,512,512]{2,1,0:T(8,128)(2,1)S(1)} %fusion.30.rest_ref, bf16[1024,128]{1,0:T(8,128)(2,1)S(1)} %compare_convert_fusion.seen_ref, bf16[1024,128]{1,0:T(8,128)(2,1)S(1)} %select_convert_fusion.bar_ref), custom_call_target="tpu_custom_call" | custom-call | flops 2097152 | bytes 2048 | tf_op jit(solution)/shard_map/attn_forward/pallas_call | solution.py:137
  57.8 8.4 %attn_forward.3 = (bf16[1024,512]{1,0:T(8,128)(2,1)S(1)}, f32[4,8,1024]{2,1,0:T(8,128)S(1)}) custom-call(bf16[3,512,512]{2,1,0:T(8,128)(2,1)S(1)} %fusion.29.own_ref, bf16[3,512,512]{2,1,0:T(8,128)(2,1)S(1)} %fusion.30.rest_ref, bf16[1024,128]{1,0:T(8,128)(2,1)S(1)} %compare_convert_fusion.seen_ref, ...), custom_call_target="tpu_custom_call", output_to_operand_aliasing={{0}: (4, {}), {1}: (5, {})} | custom-call | flops 2097152 | bytes 2048 | tf_op jit(solution)/shard_map/attn_forward/pallas_call | solution.py:137
  69.8 11.0 %collective-permute-done.5 = bf16[512,512]{1,0:T(8,128)(2,1)S(1)} collective-permute-done((bf16[512,512]{1,0:T(8,128)(2,1)S(1)}, bf16[512,512]{1,0:T(8,128)(2,1)S(1)}, u32[]{:S(2)}, u32[]{:S(2)}) %collective-permute-start.5) | collective-permute-done | bytes 524320 | tf_op jit(solution)/shard_map/ppermute | solution.py:219
  94.3 5.8 %collective-permute-done.10 = bf16[64,2048]{1,0:T(8,128)(2,1)S(1)} collective-permute-done((bf16[64,2048]{1,0:T(8,128)(2,1)S(1)}, bf16[64,2048]{1,0:T(8,128)(2,1)S(1)}, u32[]{:S(2)}, u32[]{:S(2)}) %collective-permute-start.10) | collective-permute-done | bytes 262176 | tf_op jit(solution)/shard_map/ppermute | solution.py:207
  118.9 5.6 %fusion.9 = (bf16[512,2048]{1,0:T(8,128)(2,1)}, bf16[512,2048]{1,0:T(8,128)(2,1)S(1)}) fusion(f32[2048]{0:T(1024)} %collective-permute-done.9, bf16[512,1024]{1,0:T(8,128)(2,1)S(1)} %copy-done.57, bf16[1,1024,2048]{2,1,0:T(8,128)(2,1)S(1)} %spread_rows.9), kind=kOutput, calls=%fused_computation.11 | convolution fusion | flops 2160066560 | bytes 9445376 | tf_op jit(solution)/shard_map/dot_general | solution.py:457
  146.8 6.6 %multiply_convert_fusion.1 = bf16[512,2048]{1,0:T(8,128)(2,1)} fusion(bf16[512,2048]{1,0:T(8,128)(2,1)} %get-tuple-element.151, bf16[512,1024]{1,0:T(8,128)(2,1)S(1)} %convert_element_type.391, bf16[2048,1024]{1,0:T(8,128)(2,1)} %param.22), kind=kOutput, calls=%fused_computation.28 | convolution fusion | flops 2150629376 | bytes 9437184 | tf_op jit(solution)/shard_map/sd,fd->sf/dot_general | solution.py:508
  170.5 6.7 %multiply_reduce_fusion.1 = (f32[1024]{0:T(1024)}, f32[512]{0:T(512)S(1)}, f32[512]{0:T(512)S(1)}, f32[1024]{0:T(1024)}, f32[512,1024]{1,0:T(8,128)S(1)}) fusion(f32[512,1024]{1,0:T(8,128)S(1)} %copy-done.27, f32[512]{0:T(512)S(1)} %copy-done.67, f32[512]{0:T(512)S(1)} %broadcast_multiply_fusion.5, f32[1024]{0:T(1024)S(1)} %bitcast.164, ...), kind=kOutput, calls=%fused_computation.54 | convolution fusion | flops 2153247744 | bytes 14700544 | tf_op jit(solution)/shard_map/sf,df->sd/dot_general | solution.py:518
  187.3 8.4 %collective-permute-done.22.up_rest_ref = bf16[512,512]{1,0:T(8,128)(2,1)S(1)} collective-permute-done((bf16[512,512]{1,0:T(8,128)(2,1)S(1)}, bf16[512,512]{1,0:T(8,128)(2,1)S(1)}, u32[]{:S(2)}, u32[]{:S(2)}) %collective-permute-start.22) | collective-permute-done | bytes 524320 | tf_op jit(solution)/shard_map/ppermute | solution.py:219
  202.0 12.0 %attn_backward.2 = (bf16[3,512,256]{2,1,0:T(8,128)(2,1)S(1)}, bf16[3,512,256]{2,1,0:T(8,128)(2,1)S(1)}) custom-call(bf16[3,512,512]{2,1,0:T(8,128)(2,1)S(1)} %fusion.29.own_ref, bf16[3,512,512]{2,1,0:T(8,128)(2,1)} %copy-done.1, bf16[512,512]{1,0:T(8,128)(2,1)S(1)} %convolution_convert_fusion.6.up_own_ref, ...), custom_call_target="tpu_custom_call" | custom-call | flops 2097152 | bytes 2048 | tf_op jit(solution)/shard_map/attn_backward/pallas_call | solution.py:167
  228.7 12.3 %attn_backward.3 = (bf16[3,512,256]{2,1,0:T(8,128)(2,1)S(1)}, bf16[3,512,256]{2,1,0:T(8,128)(2,1)S(1)}) custom-call(bf16[3,512,512]{2,1,0:T(8,128)(2,1)S(1)} %fusion.29.own_ref, bf16[3,512,512]{2,1,0:T(8,128)(2,1)} %copy-done.1, bf16[512,512]{1,0:T(8,128)(2,1)S(1)} %copy-done.23, bf16[512,512]{1,0:T(8,128)(2,1)S(1)} %copy-done.21, ...), custom_call_target="tpu_custom_call" | custom-call | flops 2097152 | bytes 2048 | tf_op jit(solution)/shard_map/attn_backward/pallas_call | solution.py:167
  252.7 48.1 %collective-permute-done.27 = bf16[1,256,2048]{2,1,0:T(8,128)(2,1)S(1)} collective-permute-done((bf16[1,256,2048]{2,1,0:T(8,128)(2,1)S(1)}, bf16[1,256,2048]{2,1,0:T(8,128)(2,1)S(1)}, u32[]{:S(2)}, u32[]{:S(2)}) %collective-permute-start.27) | collective-permute-done | bytes 1048608 | tf_op jit(solution)/shard_map/ppermute | solution.py:219
  310.8 7.3 %collective-permute-done.47 = bf16[1,128,2048]{2,1,0:T(8,128)(2,1)S(1)} collective-permute-done((bf16[1,128,2048]{2,1,0:T(8,128)(2,1)S(1)}, bf16[1,128,2048]{2,1,0:T(8,128)(2,1)S(1)}, u32[]{:S(2)}, u32[]{:S(2)}) %collective-permute-start.47) | collective-permute-done | bytes 524320 | tf_op jit(solution)/shard_map/ppermute | solution.py:207
  323.2 7.3 %collective-permute-done.48 = bf16[1,64,2048]{2,1,0:T(8,128)(2,1)S(1)} collective-permute-done((bf16[1,64,2048]{2,1,0:T(8,128)(2,1)S(1)}, bf16[1,64,2048]{2,1,0:T(8,128)(2,1)S(1)}, u32[]{:S(2)}, u32[]{:S(2)}) %collective-permute-start.48) | collective-permute-done | bytes 262176 | tf_op jit(solution)/shard_map/ppermute | solution.py:207
  336.6 7.8 %collective-permute-done.49 = bf16[1,64,2048]{2,1,0:T(8,128)(2,1)S(1)} collective-permute-done((bf16[1,64,2048]{2,1,0:T(8,128)(2,1)S(1)}, bf16[1,64,2048]{2,1,0:T(8,128)(2,1)S(1)}, u32[]{:S(2)}, u32[]{:S(2)}) %collective-permute-start.49) | collective-permute-done | bytes 262176 | tf_op jit(solution)/shard_map/ppermute | solution.py:207
  351.4 12.8 %collective-permute-done.50 = bf16[1,128,2048]{2,1,0:T(8,128)(2,1)} collective-permute-done((bf16[1,128,2048]{2,1,0:T(8,128)(2,1)}, bf16[1,128,2048]{2,1,0:T(8,128)(2,1)}, u32[]{:S(2)}, u32[]{:S(2)}) %collective-permute-start.50) | collective-permute-done | bytes 524320 | tf_op jit(solution)/shard_map/ppermute | solution.py:207
  366.3 16.8 %collective-permute-done.32 = bf16[3,256,256]{2,1,0:T(8,128)(2,1)S(1)} collective-permute-done((bf16[3,256,256]{2,1,0:T(8,128)(2,1)S(1)}, bf16[3,256,256]{2,1,0:T(8,128)(2,1)S(1)}, u32[]{:S(2)}, u32[]{:S(2)}) %collective-permute-start.32) | collective-permute-done | bytes 393248 | tf_op jit(solution)/shard_map/ppermute | solution.py:207
  384.5 25.9 %collective-permute-done.41 = bf16[3,64,256]{2,1,0:T(8,128)(2,1)S(1)} collective-permute-done((bf16[3,64,256]{2,1,0:T(8,128)(2,1)S(1)}, bf16[3,64,256]{2,1,0:T(8,128)(2,1)S(1)}, u32[]{:S(2)}, u32[]{:S(2)}) %collective-permute-start.41) | collective-permute-done | bytes 98336 | tf_op jit(solution)/shard_map/ppermute | solution.py:207
  415.5 10.9 %collective-permute-done.34 = bf16[3,64,256]{2,1,0:T(8,128)(2,1)S(1)} collective-permute-done((bf16[3,64,256]{2,1,0:T(8,128)(2,1)S(1)}, bf16[3,64,256]{2,1,0:T(8,128)(2,1)S(1)}, u32[]{:S(2)}, u32[]{:S(2)}) %collective-permute-start.34) | collective-permute-done | bytes 98336 | tf_op jit(solution)/shard_map/ppermute | solution.py:207
  428.5 5.5 %collective-permute-done.35 = bf16[3,64,256]{2,1,0:T(8,128)(2,1)S(1)} collective-permute-done((bf16[3,64,256]{2,1,0:T(8,128)(2,1)S(1)}, bf16[3,64,256]{2,1,0:T(8,128)(2,1)S(1)}, u32[]{:S(2)}, u32[]{:S(2)}) %collective-permute-start.35) | collective-permute-done | bytes 98336 | tf_op jit(solution)/shard_map/ppermute | solution.py:207
  441.8 11.1 %collective-permute-done.44 = bf16[3,256,256]{2,1,0:T(8,128)(2,1)S(1)} collective-permute-done((bf16[3,256,256]{2,1,0:T(8,128)(2,1)S(1)}, bf16[3,256,256]{2,1,0:T(8,128)(2,1)S(1)}, u32[]{:S(2)}, u32[]{:S(2)}) %collective-permute-start.44) | collective-permute-done | bytes 393248 | tf_op jit(solution)/shard_map/ppermute | solution.py:207
  469.6 25.2 %all-reduce.3.cloned.1.call-done = (bf16[1,1024,1024]{2,1,0:T(8,128)(2,1)}, bf16[1,256,1024]{2,1,0:T(8,128)(2,1)}) async-done(((bf16[1,1024,1024]{2,1,0:T(8,128)(2,1)}, bf16[1,256,1024]{2,1,0:T(8,128)(2,1)}), (bf16[1,1024,1024]{2,1,0:T(8,128)(2,1)}, bf16[1,256,1024]{2,1,0:T(8,128)(2,1)})) %all-reduce.3.cloned.1.call-update) | async-done | bytes 2621456 | tf_op jit(solution)/shard_map/psum | solution.py:591
  515.4 5.8 %collective-permute-done.28 = bf16[512,1024]{1,0:T(8,128)(2,1)S(1)} collective-permute-done((bf16[512,1024]{1,0:T(8,128)(2,1)}, bf16[512,1024]{1,0:T(8,128)(2,1)S(1)}, u32[]{:S(2)}, u32[]{:S(2)}) %collective-permute-start.28) | collective-permute-done | bytes 1048608 | tf_op jit(solution)/shard_map/ppermute | solution.py:219
  528.5 6.6 %spread_rows.15 = f32[1,2048,1024]{2,1,0:T(8,128)} custom-call(s32[5]{0:T(128)S(1)} %pad_add_fusion.1.order_ref, bf16[1,1024,1024]{2,1,0:T(8,128)(2,1)S(1)} %copy-done.19, bf16[1,1024,1024]{2,1,0:T(8,128)(2,1)} %collective-permute-done.60.far_ref), custom_call_target="tpu_custom_call" | custom-call | bytes 12582912 | tf_op jit(solution)/shard_map/spread_rows/pallas_call | solution.py:260
  (435 shorter events, 234.9 us)
Async XLA Ops:
  7.2 487.7 %all-reduce.3.cloned.1.call-start = ((), (), s32[]{:S(2)}) async-start(), calls=%async_computation | async-start | bytes 5242880 | tf_op jit(solution)/shard_map/psum | solution.py:591
  7.2 26.6 %collective-permute-start = (bf16[512,1024]{1,0:T(8,128)(2,1)}, bf16[512,1024]{1,0:T(8,128)(2,1)}, u32[]{:S(2)}, u32[]{:S(2)}) collective-permute-start(bf16[512,1024]{1,0:T(8,128)(2,1)} %param.12), channel_id=1, source_target_pairs={{1,0},{0,1},{3,2},{2,3},{5,4},{4,5},{7,6},{6,7},{9,8},{8,9},{11,10... | collective-permute-start | bytes 3145736 | tf_op jit(solution)/shard_map/ppermute | solution.py:212
  10.2 58.4 %collective-permute-start.9 = (f32[2048]{0:T(1024)}, f32[2048]{0:T(1024)}, u32[]{:S(2)}, u32[]{:S(2)}) collective-permute-start(f32[2048]{0:T(1024)} %param.21), channel_id=1, source_target_pairs={{1,0},{0,1},{3,2},{2,3},{5,4},{4,5},{7,6},{6,7},{9,8},{8,9},{11,10... | collective-permute-start | bytes 24584 | tf_op jit(solution)/shard_map/ppermute | solution.py:212
  68.7 25.6 %collective-permute-start.12 = (bf16[256,1024]{1,0:T(8,128)(2,1)S(1)}, bf16[256,1024]{1,0:T(8,128)(2,1)S(1)}, u32[]{:S(2)}, u32[]{:S(2)}) collective-permute-start(bf16[256,1024]{1,0:T(8,128)(2,1)S(1)} %collective-permute-done.4), channel_id=1, source_target_pairs={{0,4},{2,6},{4,0},{6,2},{8,12},{10,14},{12,8},{14,10},{16,20},{18,... | collective-permute-start | bytes 1572872 | tf_op jit(solution)/shard_map/ppermute | solution.py:207
  69.3 25.1 %collective-permute-start.13 = (bf16[256,1024]{1,0:T(8,128)(2,1)S(1)}, bf16[256,1024]{1,0:T(8,128)(2,1)S(1)}, u32[]{:S(2)}, u32[]{:S(2)}) collective-permute-start(bf16[256,1024]{1,0:T(8,128)(2,1)S(1)} %collective-permute-done.4), channel_id=1, source_target_pairs={{0,8},{2,10},{4,12},{6,14},{8,0},{10,2},{12,4},{14,6},{16,24},{18,... | collective-permute-start | bytes 1572872 | tf_op jit(solution)/shard_map/ppermute | solution.py:207
  166.0 29.7 %collective-permute-start.21 = (bf16[1,512,2048]{2,1,0:T(8,128)(2,1)S(1)}, bf16[1,512,2048]{2,1,0:T(8,128)(2,1)S(1)}, u32[]{:S(2)}, u32[]{:S(2)}) collective-permute-start(bf16[1,512,2048]{2,1,0:T(8,128)(2,1)S(1)} %dynamic-slice_bitcast_fusion), channel_id=1, source_target_pairs={{0,2},{2,0},{4,6},{6,4},{8,10},{10,8},{12,14},{14,12},{16,18},{18,... | collective-permute-start | bytes 6291464 | tf_op jit(solution)/shard_map/ppermute | solution.py:207
  170.0 25.7 %collective-permute-start.20 = (bf16[1,512,2048]{2,1,0:T(8,128)(2,1)S(1)}, bf16[1,512,2048]{2,1,0:T(8,128)(2,1)S(1)}, u32[]{:S(2)}, u32[]{:S(2)}) collective-permute-start(bf16[1,512,2048]{2,1,0:T(8,128)(2,1)S(1)} %dynamic-slice_bitcast_fusion.1), channel_id=1, source_target_pairs={{0,2},{2,0},{4,6},{6,4},{8,10},{10,8},{12,14},{14,12},{16,18},{18,... | collective-permute-start | bytes 6291464 | tf_op jit(solution)/shard_map/ppermute | solution.py:207
  201.5 39.6 %collective-permute-start.26 = (bf16[1,256,2048]{2,1,0:T(8,128)(2,1)}, bf16[1,256,2048]{2,1,0:T(8,128)(2,1)}, u32[]{:S(2)}, u32[]{:S(2)}) collective-permute-start(bf16[1,256,2048]{2,1,0:T(8,128)(2,1)} %fusion.22), channel_id=1, source_target_pairs={{0,8},{2,10},{4,12},{6,14},{8,0},{10,2},{12,4},{14,6},{16,24},{18,... | collective-permute-start | bytes 3145736 | tf_op jit(solution)/shard_map/ppermute | solution.py:207
  218.7 26.4 %collective-permute-start.25 = (bf16[3,512,256]{2,1,0:T(8,128)(2,1)}, bf16[3,512,256]{2,1,0:T(8,128)(2,1)}, u32[]{:S(2)}, u32[]{:S(2)}) collective-permute-start(bf16[3,512,256]{2,1,0:T(8,128)(2,1)} %get-tuple-element.227), channel_id=1, source_target_pairs={{0,2},{2,0},{4,6},{6,4},{8,10},{10,8},{12,14},{14,12},{16,18},{18,... | collective-permute-start | bytes 2359304 | tf_op jit(solution)/shard_map/ppermute | solution.py:207
  218.8 92.0 %collective-permute-start.29 = (bf16[1,1024,1024]{2,1,0:T(8,128)(2,1)}, bf16[1,1024,1024]{2,1,0:T(8,128)(2,1)S(1)}, u32[]{:S(2)}, u32[]{:S(2)}) collective-permute-start(bf16[1,1024,1024]{2,1,0:T(8,128)(2,1)} %fusion.10), channel_id=1, source_target_pairs={{0,1},{1,0},{2,3},{3,2},{4,5},{5,4},{6,7},{7,6},{8,9},{9,8},{10,11... | collective-permute-start | bytes 6291464 | tf_op jit(solution)/shard_map/ppermute | solution.py:219
  220.3 80.5 %collective-permute-start.46 = (bf16[1,256,2048]{2,1,0:T(8,128)(2,1)}, bf16[1,256,2048]{2,1,0:T(8,128)(2,1)}, u32[]{:S(2)}, u32[]{:S(2)}) collective-permute-start(bf16[1,256,2048]{2,1,0:T(8,128)(2,1)} %fusion.23), channel_id=1, source_target_pairs={{0,8},{2,10},{4,12},{6,14},{8,0},{10,2},{12,4},{14,6},{16,24},{18,... | collective-permute-start | bytes 3145736 | tf_op jit(solution)/shard_map/ppermute | solution.py:207
  224.2 86.6 %collective-permute-start.30 = (bf16[1,256,1024]{2,1,0:T(8,128)(2,1)}, bf16[1,256,1024]{2,1,0:T(8,128)(2,1)S(1)}, u32[]{:S(2)}, u32[]{:S(2)}) collective-permute-start(bf16[1,256,1024]{2,1,0:T(8,128)(2,1)} %fusion.38), channel_id=1, source_target_pairs={{0,1},{1,0},{2,3},{3,2},{4,5},{5,4},{6,7},{7,6},{8,9},{9,8},{10,11... | collective-permute-start | bytes 1572872 | tf_op jit(solution)/shard_map/ppermute | solution.py:219
  243.6 57.2 %collective-permute-start.27 = (bf16[1,256,2048]{2,1,0:T(8,128)(2,1)S(1)}, bf16[1,256,2048]{2,1,0:T(8,128)(2,1)S(1)}, u32[]{:S(2)}, u32[]{:S(2)}) collective-permute-start(bf16[1,256,2048]{2,1,0:T(8,128)(2,1)S(1)} %add_convert_fusion.8), channel_id=1, source_target_pairs={{0,1},{1,0},{2,3},{3,2},{4,5},{5,4},{6,7},{7,6},{8,9},{9,8},{10,11... | collective-permute-start | bytes 3145736 | tf_op jit(solution)/shard_map/ppermute | solution.py:219
  305.8 24.9 %collective-permute-start.39 = (bf16[3,256,256]{2,1,0:T(8,128)(2,1)S(1)}, bf16[3,256,256]{2,1,0:T(8,128)(2,1)S(1)}, u32[]{:S(2)}, u32[]{:S(2)}) collective-permute-start(bf16[3,256,256]{2,1,0:T(8,128)(2,1)S(1)} %add_convert_fusion.13), channel_id=1, source_target_pairs={{0,4},{2,6},{4,0},{6,2},{8,12},{10,14},{12,8},{14,10},{16,20},{18,... | collective-permute-start | bytes 1179656 | tf_op jit(solution)/shard_map/ppermute | solution.py:207
  310.8 38.1 %collective-permute-start.31 = (bf16[3,512,256]{2,1,0:T(8,128)(2,1)}, bf16[3,512,256]{2,1,0:T(8,128)(2,1)}, u32[]{:S(2)}, u32[]{:S(2)}) collective-permute-start(bf16[3,512,256]{2,1,0:T(8,128)(2,1)} %dynamic-slice_bitcast_fusion.4), channel_id=1, source_target_pairs={{0,2},{2,0},{4,6},{6,4},{8,10},{10,8},{12,14},{14,12},{16,18},{18,... | collective-permute-start | bytes 2359304 | tf_op jit(solution)/shard_map/ppermute | solution.py:207
  350.2 32.9 %collective-permute-start.32 = (bf16[3,256,256]{2,1,0:T(8,128)(2,1)S(1)}, bf16[3,256,256]{2,1,0:T(8,128)(2,1)S(1)}, u32[]{:S(2)}, u32[]{:S(2)}) collective-permute-start(bf16[3,256,256]{2,1,0:T(8,128)(2,1)S(1)} %fusion.50), channel_id=1, source_target_pairs={{0,8},{2,10},{4,12},{6,14},{8,0},{10,2},{12,4},{14,6},{16,24},{18,... | collective-permute-start | bytes 1179656 | tf_op jit(solution)/shard_map/ppermute | solution.py:207
  365.5 48.6 %collective-permute-start.51 = (bf16[1,256,2048]{2,1,0:T(8,128)(2,1)S(1)}, bf16[1,256,2048]{2,1,0:T(8,128)(2,1)S(1)}, u32[]{:S(2)}, u32[]{:S(2)}) collective-permute-start(bf16[1,256,2048]{2,1,0:T(8,128)(2,1)S(1)} %pad_maximum_fusion.1), channel_id=1, source_target_pairs={{0,8},{2,10},{4,12},{6,14},{8,0},{10,2},{12,4},{14,6},{16,24},{18,... | collective-permute-start | bytes 3145736 | tf_op jit(solution)/shard_map/ppermute | solution.py:207
  365.6 44.8 %collective-permute-start.41 = (bf16[3,64,256]{2,1,0:T(8,128)(2,1)S(1)}, bf16[3,64,256]{2,1,0:T(8,128)(2,1)S(1)}, u32[]{:S(2)}, u32[]{:S(2)}) collective-permute-start(bf16[3,64,256]{2,1,0:T(8,128)(2,1)S(1)} %constant_dynamic-slice_fusion.2), channel_id=1, source_target_pairs={{0,16},{2,18},{4,20},{6,22},{8,24},{10,26},{12,28},{14,30},{16,0},... | collective-permute-start | bytes 294920 | tf_op jit(solution)/shard_map/ppermute | solution.py:207
  384.4 29.5 %collective-permute-start.33 = (bf16[3,128,256]{2,1,0:T(8,128)(2,1)S(1)}, bf16[3,128,256]{2,1,0:T(8,128)(2,1)S(1)}, u32[]{:S(2)}, u32[]{:S(2)}) collective-permute-start(bf16[3,128,256]{2,1,0:T(8,128)(2,1)S(1)} %constant_dynamic-slice_fusion.5), channel_id=1, source_target_pairs={{0,4},{2,6},{4,0},{6,2},{8,12},{10,14},{12,8},{14,10},{16,20},{18,... | collective-permute-start | bytes 589832 | tf_op jit(solution)/shard_map/ppermute | solution.py:207
  415.4 50.0 %collective-permute-start.52 = (bf16[1,512,2048]{2,1,0:T(8,128)(2,1)S(1)}, bf16[1,512,2048]{2,1,0:T(8,128)(2,1)S(1)}, u32[]{:S(2)}, u32[]{:S(2)}) collective-permute-start(bf16[1,512,2048]{2,1,0:T(8,128)(2,1)S(1)} %pad_maximum_fusion.near_ref), channel_id=1, source_target_pairs={{0,2},{2,0},{4,6},{6,4},{8,10},{10,8},{12,14},{14,12},{16,18},{18,... | collective-permute-start | bytes 6291464 | tf_op jit(solution)/shard_map/ppermute | solution.py:207
  455.0 40.4 %collective-permute-start.53 = (f32[6144]{0:T(1024)S(1)}, f32[6144]{0:T(1024)S(1)}, u32[]{:S(2)}, u32[]{:S(2)}) collective-permute-start(f32[6144]{0:T(1024)S(1)} %constant_dynamic-update-slice_fusion.13), channel_id=1, source_target_pairs={{0,1},{1,0},{2,3},{3,2},{4,5},{5,4},{6,7},{7,6},{8,9},{9,8},{10,11... | collective-permute-start | bytes 73736 | tf_op jit(solution)/shard_map/ppermute | solution.py:347
  459.5 35.8 %collective-permute-start.54 = (f32[2048]{0:T(1024)S(1)}, f32[2048]{0:T(1024)S(1)}, u32[]{:S(2)}, u32[]{:S(2)}) collective-permute-start(f32[2048]{0:T(1024)S(1)} %convert_reduce_fusion), channel_id=1, source_target_pairs={{0,1},{1,0},{2,3},{3,2},{4,5},{5,4},{6,7},{7,6},{8,9},{9,8},{10,11... | collective-permute-start | bytes 24584 | tf_op jit(solution)/shard_map/ppermute | solution.py:219
  494.8 33.6 %collective-permute-start.60 = (bf16[1,1024,1024]{2,1,0:T(8,128)(2,1)}, bf16[1,1024,1024]{2,1,0:T(8,128)(2,1)}, u32[]{:S(2)}, u32[]{:S(2)}) collective-permute-start(bf16[1,1024,1024]{2,1,0:T(8,128)(2,1)} %get-tuple-element.202.near_ref), channel_id=1, source_target_pairs={{0,2},{2,0},{4,6},{6,4},{8,10},{10,8},{12,14},{14,12},{16,18},{18,... | collective-permute-start | bytes 6291464 | tf_op jit(solution)/shard_map/ppermute | solution.py:207
  495.3 25.8 %collective-permute-start.28 = (bf16[512,1024]{1,0:T(8,128)(2,1)}, bf16[512,1024]{1,0:T(8,128)(2,1)S(1)}, u32[]{:S(2)}, u32[]{:S(2)}) collective-permute-start(bf16[512,1024]{1,0:T(8,128)(2,1)} %fusion.24), channel_id=1, source_target_pairs={{0,1},{1,0},{2,3},{3,2},{4,5},{5,4},{6,7},{7,6},{8,9},{9,8},{10,11... | collective-permute-start | bytes 3145736 | tf_op jit(solution)/shard_map/ppermute | solution.py:219
  (119 other events, 1670.2 us)
Sparse Core Ops, SparseCore 0:
  349.0 145.7 all-reduce.2

commit v3 on v1

--- a/solution.py
+++ b/solution.py
@@ -153,9 +153,7 @@
         input_output_aliases={4: 0, 5: 1} if previous else {},
         compiler_params=pltpu.CompilerParams(vmem_limit_bytes=VMEM_ASK),
         cost_estimate=pl.CostEstimate(
-            flops=count * 16 * 256 * rows * rows,
-            transcendentals=count * 2 * rows * rows,
-            bytes_accessed=count * 10 * 128 * rows,
+            flops=count * rows * rows, transcendentals=0, bytes_accessed=count * rows
         ),
         name="attn_forward",
     )(own, rest, seen, bar, *previous)
@@ -401,11 +399,7 @@
         )
 
     out_place = 2 * bit_of(dp_pos, 1) + bit_of(dp_pos, 2)
-    out_first, up_first, down_first = (
-        slice_from(out_own, 4, out_place),
-        slice_from(up_own, 8, place),
-        slice_from(down_own, 8, place),
-    )
+    out_first, up_first = slice_from(out_own, 4, out_place), slice_from(up_own, 8, place)
     docs = [
         lax.dynamic_slice_in_dim(
             doc_ids, lax.rem(tensor_pos + ahead, ranks) * rows_own, rows_own, 0
@@ -420,26 +414,30 @@
         return (wide + bias).astype(low)
 
     qkv_own, qkv_rest = project(tokens), project(rest)
+    qkv_rest, down_own, out_first = meet(qkv_rest, down_own, out_first)
+    down_first = slice_from(down_own, 8, place)
+    out_second = send(out_first, 2)
     pairs = width // 128
     early = max(1, pairs // 2)
     block = min(512, rows_own)
     mixed_lse = attn_forward(qkv_own, qkv_rest, seen, bar, scale, block, 0, early)
-    mixed_lse, out_first, up_first = meet(mixed_lse, out_first, up_first)
-    out_second = send(out_first, 2)
+    mixed_lse, out_second, up_first = meet(mixed_lse, out_second, up_first)
     up_second, up_third = send(up_first, 2), send(up_first, 4)
     if pairs > early:
         mixed_lse = attn_forward(
             qkv_own, qkv_rest, seen, bar, scale, block, early, pairs - early, tuple(mixed_lse)
         )
-    mixed_lse, out_second, down_first = meet(mixed_lse, out_second, down_first)
     out_half = joined([out_first, out_second])
     out_far = send(out_half, 1)
+    mixed_lse, down_first = meet(mixed_lse, down_first)
     down_second, down_third = send(down_first, 2), send(down_first, 4)
     mixed, lse = mixed_lse
     mixed_parts = [mixed[k * rows_own : (k + 1) * rows_own] for k in range(ranks)]
     mixed_got = exchange(mixed_parts)
     mixed_got[0] = mixed_parts[0]
-    mixed_got, out_far, up_second, up_third = meet(mixed_got, out_far, up_second, up_third)
+    mixed_got, out_far, up_second, up_third, up_biases = meet(
+        mixed_got, out_far, up_second, up_third, up_biases
+    )
     up_corner = corner(up_second, up_third)
     outs = [out_own] + [
         spread(near, far, out_place, 1, low) for near, far in zip(out_half, out_far, strict=True)
@@ -459,28 +457,27 @@
         density = jnp.exp(-0.5 * hidden * hidden) * GAUSS_NORM
         return meet((hidden * below).astype(low), (below + hidden * density).astype(low))
 
-    normed_low, up_corner, down_second, down_third = meet(
-        normed_low, up_corner, down_second, down_third
+    pairs_active = [activate(up_own, up_bias)]
+    pairs_active, up_corner, down_second, down_third = meet(
+        pairs_active, up_corner, down_second, down_third
     )
     up_half = joined([up_first, up_second, up_third, *up_corner])
     up_far = send(up_half, 1)
     down_corner = corner(down_second, down_third)
-    pairs_active = [activate(up_own, up_bias)]
-    pairs_active, up_far = meet(pairs_active, up_far)
+    branch = jnp.dot(pairs_active[0][0], down_own, preferred_element_type=jnp.float32)
+    branch, up_far, down_corner = meet(branch, up_far, down_corner)
+    down_half = joined([down_first, down_second, down_third, *down_corner])
+    down_far = send(down_half, 1)
     ups = [up_own] + [
         spread(near, far, place, 2, low) for near, far in zip(up_half, up_far, strict=True)
     ]
-    ups, down_corner = meet(ups, down_corner)
-    down_half = joined([down_first, down_second, down_third, *down_corner])
-    down_far = send(down_half, 1)
     pairs_active += [activate(ups[k], up_biases[k]) for k in others]
     pairs_active, down_far = meet(pairs_active, down_far)
     downs = [down_own] + [
         spread(near, far, place, 2, low) for near, far in zip(down_half, down_far, strict=True)
     ]
     active, slope = zip(*pairs_active, strict=True)
-    branch = 0.0
-    for k in range(ranks):
+    for k in others:
         branch = branch + jnp.dot(active[k], downs[k], preferred_element_type=jnp.float32)
     result, unit_second, inverse_second = norm_forward(
         normed + branch + out_biases[1], ln_gains[1], ln_shifts[1]

time: 512 us -> 501 us (0.979)
  local copies, waits for them, and re-layouts: 51.9 us -> 46.2 us
    ppermute x7, waiting for transfers between devices: 9.09 us -> 16.5 us  [exchange(): lax.ppermute(parts[ahead], 'tensor', [(i, (i + ahead) % size) for i in ra...]
    unnamed x155 -> x169, local copies, waits for them, and re-layouts: 22.1 us -> 19.8 us
  transfers between devices with their start and end apart: 71 -> 71, of which waited for: 27 -> 27; matrix products, arithmetic and copies ran while one was open for 25% -> 24% of each run, Pallas kernels for 12% -> 12%
where the time goes in v3:
time: 501 us; the launch traced here: 496 us
  waiting for transfers between devices  180 us (36%)
  Pallas kernels  71 us (14%)
  matrix products  70 us (14%)
  starting transfers between devices  68.6 us (14%)
  other arithmetic  57.9 us (12%)
  local copies, waits for them, and re-layouts  46.2 us (9%)
    ppermute x50, waiting for transfers between devices, xor_step(): return lax.ppermute(array, 'dp', [(i, i ^ mask) for i in range(size)])  142 us
    ppermute x50, starting transfers between devices, xor_step(): return lax.ppermute(array, 'dp', [(i, i ^ mask) for i in range(size)])  44.6 us
    pallas_call x7, Pallas kernels, spread(): pl.pallas_call(functools.partial(spread_kernel, count), grid_spec=pltpu.P...  29.4 us
    pallas_call x2, Pallas kernels, attn_backward(): pl.pallas_call(functools.partial(attn_backward_kernel, block, scale), gri...  24.3 us
    convert_element_type x19, other arithmetic, add(): (a.astype(jnp.float32) + b.astype(jnp.float32)).astype(a.dtype)  23.5 us
    unnamed x169, local copies, waits for them, and re-layouts  19.8 us
    ppermute x5, waiting for transfers between devices, from_rank(): lax.ppermute(array, 'tensor', [((i + ahead) % size, i) for i in range(siz...  18.5 us
    pallas_call x2, Pallas kernels, attn_forward(): pl.pallas_call(functools.partial(attn_forward_kernel, block, scale), grid...  17.3 us
  transfers between devices with their start and end apart: 71, of which 27 were waited for; matrix products, arithmetic and copies ran while one was open for 24% of the time, Pallas kernels for 12%

profile of v3, /device:TPU:0, one launch (start us, length us, event | category | flops | bytes accessed | tf_op | source)
XLA Modules:
  0.0 495.8 jit_solution(15556771775025686015)
XLA Ops:
  11.7 15.5 %collective-permute-done = bf16[512,1024]{1,0:T(8,128)(2,1)} collective-permute-done((bf16[512,1024]{1,0:T(8,128)(2,1)}, bf16[512,1024]{1,0:T(8,128)(2,1)}, u32[]{:S(2)}, u32[]{:S(2)}) %collective-permute-start) | collective-permute-done | bytes 1048608 | tf_op jit(solution)/shard_map/ppermute | solution.py:216
  41.6 8.8 %attn_forward.2 = (bf16[1024,512]{1,0:T(8,128)(2,1)S(1)}, f32[4,8,1024]{2,1,0:T(8,128)S(1)}) custom-call(bf16[3,512,512]{2,1,0:T(8,128)(2,1)S(1)} %fusion.15.own_ref, bf16[3,512,512]{2,1,0:T(8,128)(2,1)S(1)} %fusion.16.rest_ref, bf16[1024,128]{1,0:T(8,128)(2,1)S(1)} %compare_convert_fusion.seen_ref, bf16[1024,128]{1,0:T(8,128)(2,1)S(1)} %select_convert_fusion.bar_ref), custom_call_target="tpu_custom_call" | custom-call | flops 2097152 | bytes 2048 | tf_op jit(solution)/shard_map/attn_forward/pallas_call | solution.py:135
  52.8 8.4 %attn_forward.3 = (bf16[1024,512]{1,0:T(8,128)(2,1)S(1)}, f32[4,8,1024]{2,1,0:T(8,128)S(1)}) custom-call(bf16[3,512,512]{2,1,0:T(8,128)(2,1)S(1)} %fusion.15.own_ref, bf16[3,512,512]{2,1,0:T(8,128)(2,1)S(1)} %fusion.16.rest_ref, bf16[1024,128]{1,0:T(8,128)(2,1)S(1)} %compare_convert_fusion.seen_ref, ...), custom_call_target="tpu_custom_call", output_to_operand_aliasing={{0}: (4, {}), {1}: (5, {})} | custom-call | flops 2097152 | bytes 2048 | tf_op jit(solution)/shard_map/attn_forward/pallas_call | solution.py:135
  64.1 11.6 %collective-permute-done.5 = bf16[512,512]{1,0:T(8,128)(2,1)S(1)} collective-permute-done((bf16[512,512]{1,0:T(8,128)(2,1)S(1)}, bf16[512,512]{1,0:T(8,128)(2,1)S(1)}, u32[]{:S(2)}, u32[]{:S(2)}) %collective-permute-start.5) | collective-permute-done | bytes 524320 | tf_op jit(solution)/shard_map/ppermute | solution.py:223
  81.9 5.1 %fusion.4 = (bf16[512,2048]{1,0:T(8,128)(2,1)}, bf16[512,2048]{1,0:T(8,128)(2,1)S(1)}) fusion(f32[2048]{0:T(1024)S(1)} %copy-done.76, bf16[512,1024]{1,0:T(8,128)(2,1)S(1)} %fusion.14, bf16[1024,2048]{1,0:T(8,128)(2,1)S(1)} %copy-done.62), kind=kOutput, calls=%fused_computation.7 | convolution fusion | flops 2160066560 | bytes 9445376 | tf_op jit(solution)/shard_map/dot_general | solution.py:455
  89.3 5.7 %collective-permute-done.10 = bf16[64,2048]{1,0:T(8,128)(2,1)S(1)} collective-permute-done((bf16[64,2048]{1,0:T(8,128)(2,1)S(1)}, bf16[64,2048]{1,0:T(8,128)(2,1)S(1)}, u32[]{:S(2)}, u32[]{:S(2)}) %collective-permute-start.10) | collective-permute-done | bytes 262176 | tf_op jit(solution)/shard_map/ppermute | solution.py:211
  113.7 5.7 %fusion.9 = (bf16[512,2048]{1,0:T(8,128)(2,1)}, bf16[512,2048]{1,0:T(8,128)(2,1)S(1)}) fusion(f32[2048]{0:T(1024)} %collective-permute-done.9, bf16[512,1024]{1,0:T(8,128)(2,1)S(1)} %copy-done.46, bf16[1024,2048]{1,0:T(8,128)(2,1)S(1)} %spread_rows.8), kind=kOutput, calls=%fused_computation.12 | convolution fusion | flops 2160066560 | bytes 9445376 | tf_op jit(solution)/shard_map/dot_general | solution.py:455
  144.4 5.7 %multiply_convert_fusion.1 = bf16[512,2048]{1,0:T(8,128)(2,1)S(1)} fusion(bf16[512,2048]{1,0:T(8,128)(2,1)} %get-tuple-element.146, bf16[512,1024]{1,0:T(8,128)(2,1)} %copy-done.42, bf16[2048,1024]{1,0:T(8,128)(2,1)} %param.22), kind=kOutput, calls=%fused_computation.16 | convolution fusion | flops 2150629376 | bytes 9437184 | tf_op jit(solution)/shard_map/sd,fd->sf/dot_general | solution.py:504
  214.4 12.1 %attn_backward.2 = (bf16[3,512,512]{2,1,0:T(8,128)(2,1)S(1)}, bf16[3,512,512]{2,1,0:T(8,128)(2,1)S(1)}) custom-call(bf16[3,512,512]{2,1,0:T(8,128)(2,1)} %copy-done.1, bf16[3,512,512]{2,1,0:T(8,128)(2,1)} %copy-done.2, bf16[512,512]{1,0:T(8,128)(2,1)S(1)} %copy-done.21, bf16[512,512]{1,0:T(8,128)(2,1)S(1)} %collective-permute-done.22.up_rest_ref, ...), custom_call_target="tpu_custom_call" | custom-call | flops 12884901888 | bytes 4718592 | tf_op jit(solution)/shard_map/attn_backward/pallas_call | solution.py:167
  230.3 18.4 %collective-permute-done.24 = bf16[512,1024]{1,0:T(8,128)(2,1)S(1)} collective-permute-done((bf16[512,1024]{1,0:T(8,128)(2,1)S(1)}, bf16[512,1024]{1,0:T(8,128)(2,1)S(1)}, u32[]{:S(2)}, u32[]{:S(2)}) %collective-permute-start.24) | collective-permute-done | bytes 1048608 | tf_op jit(solution)/shard_map/ppermute | solution.py:211
  258.1 12.3 %attn_backward.3 = (bf16[3,512,512]{2,1,0:T(8,128)(2,1)S(1)}, bf16[3,512,512]{2,1,0:T(8,128)(2,1)S(1)}) custom-call(bf16[3,512,512]{2,1,0:T(8,128)(2,1)} %copy-done.1, bf16[3,512,512]{2,1,0:T(8,128)(2,1)} %copy-done.2, bf16[512,512]{1,0:T(8,128)(2,1)S(1)} %copy-done.21, ...), custom_call_target="tpu_custom_call", output_to_operand_aliasing={{0}: (8, {}), {1}: (9, {})} | custom-call | flops 12884901888 | bytes 4718592 | tf_op jit(solution)/shard_map/attn_backward/pallas_call | solution.py:167
  285.2 4.9 copy.31
  317.4 10.5 %collective-permute-done.66 = bf16[128,1024]{1,0:T(8,128)(2,1)S(1)} collective-permute-done((bf16[128,1024]{1,0:T(8,128)(2,1)S(1)}, bf16[128,1024]{1,0:T(8,128)(2,1)S(1)}, u32[]{:S(2)}, u32[]{:S(2)}) %collective-permute-start.66) | collective-permute-done | bytes 262176 | tf_op jit(solution)/shard_map/ppermute | solution.py:211
  331.2 11.1 %collective-permute-done.36 = bf16[768,512]{1,0:T(8,128)(2,1)S(1)} collective-permute-done((bf16[768,512]{1,0:T(8,128)(2,1)S(1)}, bf16[768,512]{1,0:T(8,128)(2,1)S(1)}, u32[]{:S(2)}, u32[]{:S(2)}) %collective-permute-start.36) | collective-permute-done | bytes 786464 | tf_op jit(solution)/shard_map/ppermute | solution.py:211
  344.4 8.7 %collective-permute-done.61 = bf16[64,2048]{1,0:T(8,128)(2,1)S(1)} collective-permute-done((bf16[64,2048]{1,0:T(8,128)(2,1)S(1)}, bf16[64,2048]{1,0:T(8,128)(2,1)S(1)}, u32[]{:S(2)}, u32[]{:S(2)}) %collective-permute-start.61) | collective-permute-done | bytes 262176 | tf_op jit(solution)/shard_map/ppermute | solution.py:211
  356.4 9.6 %collective-permute-done.62 = bf16[64,2048]{1,0:T(8,128)(2,1)S(1)} collective-permute-done((bf16[64,2048]{1,0:T(8,128)(2,1)S(1)}, bf16[64,2048]{1,0:T(8,128)(2,1)S(1)}, u32[]{:S(2)}, u32[]{:S(2)}) %collective-permute-start.62) | collective-permute-done | bytes 262176 | tf_op jit(solution)/shard_map/ppermute | solution.py:211
  369.7 12.8 %collective-permute-done.68 = bf16[256,1024]{1,0:T(8,128)(2,1)S(1)} collective-permute-done((bf16[256,1024]{1,0:T(8,128)(2,1)S(1)}, bf16[256,1024]{1,0:T(8,128)(2,1)S(1)}, u32[]{:S(2)}, u32[]{:S(2)}) %collective-permute-start.68) | collective-permute-done | bytes 524320 | tf_op jit(solution)/shard_map/ppermute | solution.py:211
  385.3 8.7 %collective-permute-done.39 = bf16[192,512]{1,0:T(8,128)(2,1)S(1)} collective-permute-done((bf16[192,512]{1,0:T(8,128)(2,1)S(1)}, bf16[192,512]{1,0:T(8,128)(2,1)S(1)}, u32[]{:S(2)}, u32[]{:S(2)}) %collective-permute-start.39) | collective-permute-done | bytes 196640 | tf_op jit(solution)/shard_map/ppermute | solution.py:211
  396.9 23.1 %collective-permute-done.49 = bf16[32,1024]{1,0:T(8,128)(2,1)S(1)} collective-permute-done((bf16[32,1024]{1,0:T(8,128)(2,1)S(1)}, bf16[32,1024]{1,0:T(8,128)(2,1)S(1)}, u32[]{:S(2)}, u32[]{:S(2)}) %collective-permute-start.49) | collective-permute-done | bytes 65568 | tf_op jit(solution)/shard_map/ppermute | solution.py:211
  429.7 13.6 %collective-permute-done.41 = bf16[768,512]{1,0:T(8,128)(2,1)S(1)} collective-permute-done((bf16[768,512]{1,0:T(8,128)(2,1)S(1)}, bf16[768,512]{1,0:T(8,128)(2,1)S(1)}, u32[]{:S(2)}, u32[]{:S(2)}) %collective-permute-start.41) | collective-permute-done | bytes 786464 | tf_op jit(solution)/shard_map/ppermute | solution.py:211
  451.2 5.6 %collective-permute-done.52 = bf16[128,1024]{1,0:T(8,128)(2,1)} collective-permute-done((bf16[128,1024]{1,0:T(8,128)(2,1)}, bf16[128,1024]{1,0:T(8,128)(2,1)}, u32[]{:S(2)}, u32[]{:S(2)}) %collective-permute-start.52) | collective-permute-done | bytes 262176 | tf_op jit(solution)/shard_map/ppermute | solution.py:211
  475.9 6.9 %spread_rows.13 = f32[2048,1024]{1,0:T(8,128)} custom-call(s32[8]{0:T(128)S(1)} %pad_add_fusion.3.order_ref, bf16[1024,1024]{1,0:T(8,128)(2,1)} %pad_maximum_fusion.1.near_ref, bf16[1024,1024]{1,0:T(8,128)(2,1)} %collective-permute-done.70.far_ref), custom_call_target="tpu_custom_call" | custom-call | bytes 12582912 | tf_op jit(solution)/shard_map/spread_rows/pallas_call | solution.py:262
  482.8 5.8 %spread_rows.10 = f32[3072,512]{1,0:T(8,128)} custom-call(s32[8]{0:T(128)S(1)} %pad_add_fusion.3.order_ref, bf16[1536,512]{1,0:T(8,128)(2,1)} %pad_maximum_fusion.2.near_ref, bf16[1536,512]{1,0:T(8,128)(2,1)} %collective-permute-done.42.far_ref), custom_call_target="tpu_custom_call" | custom-call | bytes 9437184 | tf_op jit(solution)/shard_map/spread_rows/pallas_call | solution.py:262
  488.7 6.9 %spread_rows.12 = f32[1024,2048]{1,0:T(8,128)} custom-call(s32[8]{0:T(128)S(1)} %pad_add_fusion.4.order_ref, bf16[512,2048]{1,0:T(8,128)(2,1)} %pad_maximum_fusion.near_ref, bf16[512,2048]{1,0:T(8,128)(2,1)} %collective-permute-done.65.far_ref), custom_call_target="tpu_custom_call" | custom-call | bytes 12582912 | tf_op jit(solution)/shard_map/spread_rows/pallas_call | solution.py:262
  (446 shorter events, 256.1 us)
Async XLA Ops:
  0.7 26.6 %collective-permute-start = (bf16[512,1024]{1,0:T(8,128)(2,1)}, bf16[512,1024]{1,0:T(8,128)(2,1)}, u32[]{:S(2)}, u32[]{:S(2)}) collective-permute-start(bf16[512,1024]{1,0:T(8,128)(2,1)} %param.12), channel_id=1, source_target_pairs={{1,0},{0,1},{3,2},{2,3},{5,4},{4,5},{7,6},{6,7},{9,8},{8,9},{11,10... | collective-permute-start | bytes 3145736 | tf_op jit(solution)/shard_map/ppermute | solution.py:216
  3.7 58.4 %collective-permute-start.9 = (f32[2048]{0:T(1024)}, f32[2048]{0:T(1024)}, u32[]{:S(2)}, u32[]{:S(2)}) collective-permute-start(f32[2048]{0:T(1024)} %param.21), channel_id=1, source_target_pairs={{1,0},{0,1},{3,2},{2,3},{5,4},{4,5},{7,6},{6,7},{9,8},{8,9},{11,10... | collective-permute-start | bytes 24584 | tf_op jit(solution)/shard_map/ppermute | solution.py:216
  62.1 27.2 %collective-permute-start.12 = (bf16[256,1024]{1,0:T(8,128)(2,1)S(1)}, bf16[256,1024]{1,0:T(8,128)(2,1)S(1)}, u32[]{:S(2)}, u32[]{:S(2)}) collective-permute-start(bf16[256,1024]{1,0:T(8,128)(2,1)S(1)} %collective-permute-done.4), channel_id=1, source_target_pairs={{0,4},{2,6},{4,0},{6,2},{8,12},{10,14},{12,8},{14,10},{16,20},{18,... | collective-permute-start | bytes 1572872 | tf_op jit(solution)/shard_map/ppermute | solution.py:211
  63.6 25.7 %collective-permute-start.13 = (bf16[256,1024]{1,0:T(8,128)(2,1)S(1)}, bf16[256,1024]{1,0:T(8,128)(2,1)S(1)}, u32[]{:S(2)}, u32[]{:S(2)}) collective-permute-start(bf16[256,1024]{1,0:T(8,128)(2,1)S(1)} %collective-permute-done.4), channel_id=1, source_target_pairs={{0,8},{2,10},{4,12},{6,14},{8,0},{10,2},{12,4},{14,6},{16,24},{18,... | collective-permute-start | bytes 1572872 | tf_op jit(solution)/shard_map/ppermute | solution.py:211
  202.4 26.2 %collective-permute-start.23 = (bf16[512,1024]{1,0:T(8,128)(2,1)S(1)}, bf16[512,1024]{1,0:T(8,128)(2,1)}, u32[]{:S(2)}, u32[]{:S(2)}) collective-permute-start(bf16[512,1024]{1,0:T(8,128)(2,1)S(1)} %copy-done.50), channel_id=1, source_target_pairs={{0,4},{2,6},{4,0},{6,2},{8,12},{10,14},{12,8},{14,10},{16,20},{18,... | collective-permute-start | bytes 3145736 | tf_op jit(solution)/shard_map/ppermute | solution.py:211
  204.0 44.6 %collective-permute-start.24 = (bf16[512,1024]{1,0:T(8,128)(2,1)S(1)}, bf16[512,1024]{1,0:T(8,128)(2,1)S(1)}, u32[]{:S(2)}, u32[]{:S(2)}) collective-permute-start(bf16[512,1024]{1,0:T(8,128)(2,1)S(1)} %copy-done.49), channel_id=1, source_target_pairs={{0,4},{2,6},{4,0},{6,2},{8,12},{10,14},{12,8},{14,10},{16,20},{18,... | collective-permute-start | bytes 3145736 | tf_op jit(solution)/shard_map/ppermute | solution.py:211
  208.0 62.4 %collective-permute-start.28 = (bf16[256,2048]{1,0:T(8,128)(2,1)}, bf16[256,2048]{1,0:T(8,128)(2,1)}, u32[]{:S(2)}, u32[]{:S(2)}) collective-permute-start(bf16[256,2048]{1,0:T(8,128)(2,1)} %add_convert_fusion.13), channel_id=1, source_target_pairs={{0,8},{2,10},{4,12},{6,14},{8,0},{10,2},{12,4},{14,6},{16,24},{18,... | collective-permute-start | bytes 3145736 | tf_op jit(solution)/shard_map/ppermute | solution.py:211
  213.9 34.8 %collective-permute-start.25 = (bf16[256,1024]{1,0:T(8,128)(2,1)}, bf16[256,1024]{1,0:T(8,128)(2,1)}, u32[]{:S(2)}, u32[]{:S(2)}) collective-permute-start(bf16[256,1024]{1,0:T(8,128)(2,1)} %constant_dynamic-slice_fusion.10), channel_id=1, source_target_pairs={{0,2},{2,0},{4,6},{6,4},{8,10},{10,8},{12,14},{14,12},{16,18},{18,... | collective-permute-start | bytes 1572872 | tf_op jit(solution)/shard_map/ppermute | solution.py:211
  213.9 34.8 %collective-permute-start.26 = (bf16[256,1024]{1,0:T(8,128)(2,1)}, bf16[256,1024]{1,0:T(8,128)(2,1)}, u32[]{:S(2)}, u32[]{:S(2)}) collective-permute-start(bf16[256,1024]{1,0:T(8,128)(2,1)} %constant_dynamic-slice_fusion.9), channel_id=1, source_target_pairs={{0,2},{2,0},{4,6},{6,4},{8,10},{10,8},{12,14},{14,12},{16,18},{18,... | collective-permute-start | bytes 1572872 | tf_op jit(solution)/shard_map/ppermute | solution.py:211
  228.6 44.5 %collective-permute-start.29 = (bf16[256,2048]{1,0:T(8,128)(2,1)}, bf16[256,2048]{1,0:T(8,128)(2,1)S(1)}, u32[]{:S(2)}, u32[]{:S(2)}) collective-permute-start(bf16[256,2048]{1,0:T(8,128)(2,1)} %add_convert_fusion.12), channel_id=1, source_target_pairs={{0,8},{2,10},{4,12},{6,14},{8,0},{10,2},{12,4},{14,6},{16,24},{18,... | collective-permute-start | bytes 3145736 | tf_op jit(solution)/shard_map/ppermute | solution.py:211
  270.5 174.2 %collective-permute-start.59 = (f32[8192]{0:T(1024)}, f32[8192]{0:T(1024)}, u32[]{:S(2)}, u32[]{:S(2)}) collective-permute-start(f32[8192]{0:T(1024)} %add.571), channel_id=1, source_target_pairs={{0,16},{2,18},{4,20},{6,22},{8,24},{10,26},{12,28},{14,30},{16,0},... | collective-permute-start | bytes 98312 | tf_op jit(solution)/shard_map/ppermute | solution.py:346
  277.0 32.0 %collective-permute-start.32 = (bf16[256,2048]{1,0:T(8,128)(2,1)}, bf16[256,2048]{1,0:T(8,128)(2,1)}, u32[]{:S(2)}, u32[]{:S(2)}) collective-permute-start(bf16[256,2048]{1,0:T(8,128)(2,1)} %add_convert_fusion.10), channel_id=1, source_target_pairs={{0,1},{1,0},{2,3},{3,2},{4,5},{5,4},{6,7},{7,6},{8,9},{9,8},{10,11... | collective-permute-start | bytes 3145736 | tf_op jit(solution)/shard_map/ppermute | solution.py:223
  301.3 51.9 %collective-permute-start.47 = (bf16[128,1024]{1,0:T(8,128)(2,1)S(1)}, bf16[128,1024]{1,0:T(8,128)(2,1)S(1)}, u32[]{:S(2)}, u32[]{:S(2)}) collective-permute-start(bf16[128,1024]{1,0:T(8,128)(2,1)S(1)} %add_convert_fusion.28), channel_id=1, source_target_pairs={{0,1},{1,0},{2,3},{3,2},{4,5},{5,4},{6,7},{7,6},{8,9},{9,8},{10,11... | collective-permute-start | bytes 786440 | tf_op jit(solution)/shard_map/ppermute | solution.py:223
  316.8 25.5 %collective-permute-start.36 = (bf16[768,512]{1,0:T(8,128)(2,1)S(1)}, bf16[768,512]{1,0:T(8,128)(2,1)S(1)}, u32[]{:S(2)}, u32[]{:S(2)}) collective-permute-start(bf16[768,512]{1,0:T(8,128)(2,1)S(1)} %add_convert_fusion.20), channel_id=1, source_target_pairs={{0,4},{2,6},{4,0},{6,2},{8,12},{10,14},{12,8},{14,10},{16,20},{18,... | collective-permute-start | bytes 2359304 | tf_op jit(solution)/shard_map/ppermute | solution.py:211
  328.0 26.6 %collective-permute-start.67 = (bf16[128,1024]{1,0:T(8,128)(2,1)S(1)}, bf16[128,1024]{1,0:T(8,128)(2,1)S(1)}, u32[]{:S(2)}, u32[]{:S(2)}) collective-permute-start(bf16[128,1024]{1,0:T(8,128)(2,1)S(1)} %add_convert_fusion.25), channel_id=1, source_target_pairs={{0,16},{2,18},{4,20},{6,22},{8,24},{10,26},{12,28},{14,30},{16,0},... | collective-permute-start | bytes 786440 | tf_op jit(solution)/shard_map/ppermute | solution.py:211
  328.3 24.8 %collective-permute-start.61 = (bf16[64,2048]{1,0:T(8,128)(2,1)S(1)}, bf16[64,2048]{1,0:T(8,128)(2,1)S(1)}, u32[]{:S(2)}, u32[]{:S(2)}) collective-permute-start(bf16[64,2048]{1,0:T(8,128)(2,1)S(1)} %constant_dynamic-slice_fusion), channel_id=1, source_target_pairs={{0,16},{2,18},{4,20},{6,22},{8,24},{10,26},{12,28},{14,30},{16,0},... | collective-permute-start | bytes 786440 | tf_op jit(solution)/shard_map/ppermute | solution.py:211
  354.6 28.0 %collective-permute-start.68 = (bf16[256,1024]{1,0:T(8,128)(2,1)S(1)}, bf16[256,1024]{1,0:T(8,128)(2,1)S(1)}, u32[]{:S(2)}, u32[]{:S(2)}) collective-permute-start(bf16[256,1024]{1,0:T(8,128)(2,1)S(1)} %pad_maximum_fusion.8), channel_id=1, source_target_pairs={{0,8},{2,10},{4,12},{6,14},{8,0},{10,2},{12,4},{14,6},{16,24},{18,... | collective-permute-start | bytes 1572872 | tf_op jit(solution)/shard_map/ppermute | solution.py:211
  382.6 40.9 %collective-permute-start.69 = (bf16[512,1024]{1,0:T(8,128)(2,1)S(1)}, bf16[512,1024]{1,0:T(8,128)(2,1)S(1)}, u32[]{:S(2)}, u32[]{:S(2)}) collective-permute-start(bf16[512,1024]{1,0:T(8,128)(2,1)S(1)} %pad_maximum_fusion.4), channel_id=1, source_target_pairs={{0,4},{2,6},{4,0},{6,2},{8,12},{10,14},{12,8},{14,10},{16,20},{18,... | collective-permute-start | bytes 3145736 | tf_op jit(solution)/shard_map/ppermute | solution.py:211
  383.5 43.1 %collective-permute-start.64 = (bf16[256,2048]{1,0:T(8,128)(2,1)S(1)}, bf16[256,2048]{1,0:T(8,128)(2,1)S(1)}, u32[]{:S(2)}, u32[]{:S(2)}) collective-permute-start(bf16[256,2048]{1,0:T(8,128)(2,1)S(1)} %pad_maximum_fusion.3), channel_id=1, source_target_pairs={{0,8},{2,10},{4,12},{6,14},{8,0},{10,2},{12,4},{14,6},{16,24},{18,... | collective-permute-start | bytes 3145736 | tf_op jit(solution)/shard_map/ppermute | solution.py:211
  394.0 28.3 %collective-permute-start.40 = (bf16[384,512]{1,0:T(8,128)(2,1)S(1)}, bf16[384,512]{1,0:T(8,128)(2,1)S(1)}, u32[]{:S(2)}, u32[]{:S(2)}) collective-permute-start(bf16[384,512]{1,0:T(8,128)(2,1)S(1)} %pad_maximum_fusion.9), channel_id=1, source_target_pairs={{0,8},{2,10},{4,12},{6,14},{8,0},{10,2},{12,4},{14,6},{16,24},{18,... | collective-permute-start | bytes 1179656 | tf_op jit(solution)/shard_map/ppermute | solution.py:211
  394.1 25.8 %collective-permute-start.49 = (bf16[32,1024]{1,0:T(8,128)(2,1)S(1)}, bf16[32,1024]{1,0:T(8,128)(2,1)S(1)}, u32[]{:S(2)}, u32[]{:S(2)}) collective-permute-start(bf16[32,1024]{1,0:T(8,128)(2,1)S(1)} %constant_dynamic-slice_fusion.2), channel_id=1, source_target_pairs={{0,16},{2,18},{4,20},{6,22},{8,24},{10,26},{12,28},{14,30},{16,0},... | collective-permute-start | bytes 196616 | tf_op jit(solution)/shard_map/ppermute | solution.py:211
  426.5 49.3 %collective-permute-start.70 = (bf16[1024,1024]{1,0:T(8,128)(2,1)}, bf16[1024,1024]{1,0:T(8,128)(2,1)}, u32[]{:S(2)}, u32[]{:S(2)}) collective-permute-start(bf16[1024,1024]{1,0:T(8,128)(2,1)} %pad_maximum_fusion.1.near_ref), channel_id=1, source_target_pairs={{0,2},{2,0},{4,6},{6,4},{8,10},{10,8},{12,14},{14,12},{16,18},{18,... | collective-permute-start | bytes 6291464 | tf_op jit(solution)/shard_map/ppermute | solution.py:211
  428.0 60.7 %collective-permute-start.65 = (bf16[512,2048]{1,0:T(8,128)(2,1)}, bf16[512,2048]{1,0:T(8,128)(2,1)}, u32[]{:S(2)}, u32[]{:S(2)}) collective-permute-start(bf16[512,2048]{1,0:T(8,128)(2,1)} %pad_maximum_fusion.near_ref), channel_id=1, source_target_pairs={{0,2},{2,0},{4,6},{6,4},{8,10},{10,8},{12,14},{14,12},{16,18},{18,... | collective-permute-start | bytes 6291464 | tf_op jit(solution)/shard_map/ppermute | solution.py:211
  444.7 38.2 %collective-permute-start.42 = (bf16[1536,512]{1,0:T(8,128)(2,1)}, bf16[1536,512]{1,0:T(8,128)(2,1)}, u32[]{:S(2)}, u32[]{:S(2)}) collective-permute-start(bf16[1536,512]{1,0:T(8,128)(2,1)} %pad_maximum_fusion.2.near_ref), channel_id=1, source_target_pairs={{0,2},{2,0},{4,6},{6,4},{8,10},{10,8},{12,14},{14,12},{16,18},{18,... | collective-permute-start | bytes 4718600 | tf_op jit(solution)/shard_map/ppermute | solution.py:211
  (127 other events, 1077.9 us)
